TPU v7x, 128 devices: a whole 4x4x4 slice. The times are simulated.
128 devices in a mesh: leaf: 4 (over x), grp: 32 (over z, y, core).
Axes of the slice: x: 4, y: 4, z: 4, core: 2. Of those that a mesh axis runs over, the one named last changes fastest.
Arguments:
- rhs_leaf: float32 [4, 32768, 256], P('leaf', 'grp'), may hold values from -6 to 6
- rhs_group: float32 [4, 512, 256], P('leaf'), may hold values from -6 to 6
- rhs_middle: float32 [1024, 256], replicated, may hold values from -6 to 6
- rhs_top: float32 [1024, 256], replicated, may hold values from -6 to 6
- inv_leaf: bfloat16 [4, 256, 128, 128], P('leaf', 'grp')
- inv_group: bfloat16 [4, 512, 512], P('leaf')
- inv_middle: bfloat16 [1024, 1024], replicated
- inv_top: bfloat16 [1024, 1024], replicated
- leaf_tiles: bfloat16 [4, 8192, 128, 128], P('leaf', 'grp'), may hold values from -0.015625 to 0.015625
- tile_column: int32 [4, 8192], P('leaf', 'grp'), may hold values from 0 to 7
- tile_target: int32 [4, 8192], P('leaf', 'grp'), may hold values from 0 to 19
- tile_count: int32 [4, 32], P('leaf', 'grp'), may hold values from 64 to 256, as said below
- group_panel: bfloat16 [4, 2048, 512], P('leaf', 'grp'), may hold values from -0.125 to 0.125
- middle_panel: bfloat16 [1024, 1024], P(('leaf', 'grp')), may hold values from -0.1875 to 0.1875
Outputs:
- leaf_out: float32 [4, 32768, 256], P('leaf', 'grp')
- group_out: float32 [4, 512, 256], P('leaf')
- mid_out: float32 [1024, 256], replicated
- top_out: float32 [1024, 256], replicated
Inputs may be any that keep to these rules, and one draw needn't show every extreme that they name: Only the first tile_count slots of a device hold blocks of the factor; the other slots are ignored. Some device has all 256 slots live.
All inputs are finite; a program needn't handle non-finite values.
Results may differ from a plain program's by a relative error of at most 0.018.
Values may be sent and summed in bfloat16 or wider, within the bound.
A program may use at most 128 MiB of HBM per device.

v0:
```python
import jax
import jax.numpy as jnp
from jax import lax
from jax.sharding import PartitionSpec as P

BLOCK = 128
GROUP_COLS = 512
MID_COLS = 1024
LEAF_SN = 8
UPPER_BLOCKS = 20


tile_step = 16


def upper_forward(inverse, residual):
    return jnp.dot(
        inverse, residual.astype(jnp.bfloat16), preferred_element_type=jnp.float32
    ).astype(jnp.bfloat16)


def upper_backward(inverse, vector):
    return jnp.einsum("ji,jr->ir", inverse, vector, preferred_element_type=jnp.float32)


def solve_columns(
    rhs_leaf,
    rhs_group,
    rhs_middle,
    rhs_top,
    inv_leaf,
    inv_group,
    inv_middle,
    inv_top,
    leaf_tiles,
    tile_column,
    tile_target,
    tile_count,
    group_panel,
    middle_panel,
    whole_panels,
):
    width = rhs_top.shape[-1]
    tiles_here = leaf_tiles[0]
    columns_here = tile_column[0]
    targets_here = tile_target[0]
    live_count = tile_count[0, 0]
    trips = (live_count + tile_step - 1) // tile_step
    leaf_rhs = rhs_leaf[0].reshape(LEAF_SN, BLOCK, width).astype(jnp.bfloat16)
    leaf_solved = jnp.einsum(
        "sij,sjr->sir", inv_leaf[0], leaf_rhs, preferred_element_type=jnp.float32
    ).astype(jnp.bfloat16)

    def slot_block(step_index):
        begin = step_index * tile_step
        tile_block = lax.dynamic_slice_in_dim(tiles_here, begin, tile_step, 0)
        column_block = lax.dynamic_slice_in_dim(columns_here, begin, tile_step, 0)
        target_block = lax.dynamic_slice_in_dim(targets_here, begin, tile_step, 0)
        live_block = begin + jnp.arange(tile_step, dtype=jnp.int32) < live_count
        return (tile_block, column_block, target_block, live_block)

    def forward_step(step_index, totals):
        tile_block, column_block, target_block, live_block = slot_block(step_index)
        picked = leaf_solved[column_block]
        terms = jnp.einsum("pij,pjr->pir", tile_block, picked, preferred_element_type=jnp.float32)
        terms = jnp.where(live_block[:, None, None], terms, 0.0)
        return totals.at[target_block].add(terms)

    totals = lax.fori_loop(
        0, trips, forward_step, jnp.zeros((UPPER_BLOCKS, BLOCK, width), jnp.float32)
    )
    flat = totals.reshape(UPPER_BLOCKS * BLOCK, width)
    group_sum = lax.psum(flat[:GROUP_COLS], "grp")
    group_solved = upper_forward(inv_group[0], rhs_group[0] - group_sum)
    panel_rows = group_panel.shape[1]
    panel_begin = lax.axis_index("grp") * panel_rows
    panel_terms = jnp.dot(group_panel[0], group_solved, preferred_element_type=jnp.float32)
    upper = flat[GROUP_COLS:]
    section = lax.dynamic_slice_in_dim(upper, panel_begin, panel_rows, 0) + panel_terms
    upper = lax.dynamic_update_slice_in_dim(upper, section, panel_begin, 0)
    mid_sum = lax.psum(upper[:MID_COLS], ("leaf", "grp"))
    mid_solved = upper_forward(inv_middle, rhs_middle - mid_sum)
    middle_rows = middle_panel.shape[0]
    middle_begin = lax.axis_index(("leaf", "grp")) * middle_rows
    top_part = upper[MID_COLS:]
    top_section = lax.dynamic_slice_in_dim(top_part, middle_begin, middle_rows, 0) + jnp.dot(
        middle_panel, mid_solved, preferred_element_type=jnp.float32
    )
    top_part = lax.dynamic_update_slice_in_dim(top_part, top_section, middle_begin, 0)
    top_sum = lax.psum(top_part, ("leaf", "grp"))
    top_solved = upper_forward(inv_top, rhs_top - top_sum)
    top_out = upper_backward(inv_top, top_solved)
    top_round = top_out.astype(jnp.bfloat16)
    my_top = lax.dynamic_slice_in_dim(top_round, middle_begin, middle_rows, 0)
    mid_terms = jnp.einsum("ji,jr->ir", middle_panel, my_top, preferred_element_type=jnp.float32)
    mid_back = mid_solved.astype(jnp.float32) - lax.psum(mid_terms, ("leaf", "grp"))
    mid_out = upper_backward(inv_middle, mid_back.astype(jnp.bfloat16))
    upper_round = jnp.concatenate([mid_out.astype(jnp.bfloat16), top_round], axis=0)
    my_upper = lax.dynamic_slice_in_dim(upper_round, panel_begin, panel_rows, 0)
    group_terms = jnp.einsum(
        "ji,jr->ir", group_panel[0], my_upper, preferred_element_type=jnp.float32
    )
    group_back = group_solved.astype(jnp.float32) - lax.psum(
        group_terms.astype(jnp.bfloat16), "grp"
    ).astype(jnp.float32)
    group_out = upper_backward(inv_group[0], group_back.astype(jnp.bfloat16))
    above = jnp.concatenate([group_out.astype(jnp.bfloat16), upper_round], axis=0).reshape(
        UPPER_BLOCKS, BLOCK, width
    )

    def backward_step(step_index, totals_back):
        tile_block, column_block, target_block, live_block = slot_block(step_index)
        picked = above[target_block]
        terms = jnp.einsum("pji,pjr->pir", tile_block, picked, preferred_element_type=jnp.float32)
        terms = jnp.where(live_block[:, None, None], terms, 0.0)
        return totals_back.at[column_block].add(terms)

    leaf_terms = lax.fori_loop(
        0, trips, backward_step, jnp.zeros((LEAF_SN, BLOCK, width), jnp.float32)
    )
    leaf_back = (leaf_solved.astype(jnp.float32) - leaf_terms).astype(jnp.bfloat16)
    leaf_out = jnp.einsum(
        "sji,sjr->sir", inv_leaf[0], leaf_back, preferred_element_type=jnp.float32
    )
    return (leaf_out.reshape(1, LEAF_SN * BLOCK, width), group_out[None], mid_out, top_out)


def body(
    rhs_leaf,
    rhs_group,
    rhs_middle,
    rhs_top,
    inv_leaf,
    inv_group,
    inv_middle,
    inv_top,
    leaf_tiles,
    tile_column,
    tile_target,
    tile_count,
    group_panel,
    middle_panel,
):
    fixed_parts = (
        inv_leaf,
        inv_group,
        inv_middle,
        inv_top,
        leaf_tiles,
        tile_column,
        tile_target,
        tile_count,
        group_panel,
        middle_panel,
        None,
    )
    return solve_columns(rhs_leaf, rhs_group, rhs_middle, rhs_top, *fixed_parts)


def solution(mesh):
    placed = (
        P("leaf", "grp", None),
        P("leaf", None, None),
        P(),
        P(),
        P("leaf", "grp", None, None),
        P("leaf", None, None),
        P(),
        P(),
        P("leaf", "grp", None, None),
        P("leaf", "grp"),
        P("leaf", "grp"),
        P("leaf", "grp"),
        P("leaf", "grp", None),
        P(("leaf", "grp"), None),
    )
    return jax.shard_map(
        body,
        mesh=mesh,
        in_specs=placed,
        out_specs=(P("leaf", "grp", None), P("leaf", None, None), P(), P()),
        check_vma=False,
    )
```

profile of v0, /device:TPU:4, one launch (start us, length us, event | category | flops | bytes accessed | tf_op | source)
XLA Modules:
  0.0 1035.3 jit_solution(4830250386253013433)
XLA Ops:
  13.2 166.5 %while.20 = (s32[]{:T(128)}, f32[20,128,256]{2,1,0:T(8,128)}, s32[]{:T(128)}, s32[256]{0:T(256)S(1)}, s32[]{:T(128)}, /*index=5*/bf16[256,128,128]{2,1,0:T(8,128...) while((s32[]{:T(128)}, f32[20,128,256]{2,1,0:T(8,128)}, ...), condition=%wide.region_2.3_spmd, body=%wide.region_0.2_spmd.sunk | while | flops 135267456 | bytes 12063379 | solution.py:69
  18.4 5.1 scatter_fusion
  28.7 5.3 scatter_fusion
  39.2 5.1 scatter_fusion
  49.5 5.2 scatter_fusion
  59.9 5.2 scatter_fusion
  70.3 5.3 scatter_fusion
  80.8 5.1 scatter_fusion
  91.1 5.3 scatter_fusion
  101.6 5.3 scatter_fusion
  112.1 5.3 scatter_fusion
  122.6 5.1 scatter_fusion
  132.9 5.2 scatter_fusion
  143.3 5.2 scatter_fusion
  153.7 5.1 scatter_fusion
  164.0 5.2 scatter_fusion
  174.4 5.3 scatter_fusion
  181.7 3.2 slice.20
  184.9 103.1 %all-reduce.6.cloned.1.call-done = f32[512,256]{1,0:T(8,128)} async-done(((f32[512,256]{1,0:T(8,128)}), f32[512,256]{1,0:T(8,128)}) %all-reduce.6.cloned.1.call-update) | async-done | bytes 524304 | tf_op jit(solution)/shard_map/psum | solution.py:73
  294.1 146.9 %all-reduce.8.cloned.1.call-done = f32[1024,256]{1,0:T(8,128)} async-done(((f32[1024,256]{1,0:T(8,128)}), f32[1024,256]{1,0:T(8,128)}) %all-reduce.8.cloned.1.call-update) | async-done | bytes 1048592 | tf_op jit(solution)/shard_map/psum | solution.py:81
  444.9 148.3 %all-reduce.10.cloned.1.call-done = f32[1024,256]{1,0:T(8,128)} async-done(((f32[1024,256]{1,0:T(8,128)}), f32[1024,256]{1,0:T(8,128)}) %all-reduce.10.cloned.1.call-update) | async-done | bytes 1048592 | tf_op jit(solution)/shard_map/psum | solution.py:90
  593.2 5.1 fusion.30
  599.7 146.9 %all-reduce.12.cloned.1.call-done = f32[1024,256]{0,1:T(8,128)} async-done(((f32[1024,256]{0,1:T(8,128)}), f32[1024,256]{0,1:T(8,128)}) %all-reduce.12.cloned.1.call-update) | async-done | bytes 1048592 | tf_op jit(solution)/shard_map/psum | solution.py:96
  751.4 12.1 %copy.25 = bf16[1,256,128,128]{2,3,1,0:T(8,128)(2,1)} copy(bf16[1,256,128,128]{3,2,1,0:T(8,128)(2,1)} %bitcast.90) | data formatting | bytes 16777216 | tf_op args[8]
  767.4 86.4 %all-reduce.14.cloned.1.call-done = bf16[512,256]{0,1:T(8,128)(2,1)} async-done(((bf16[512,256]{0,1:T(8,128)(2,1)}), bf16[512,256]{0,1:T(8,128)(2,1)}) %all-reduce.14.cloned.1.call-update) | async-done | bytes 262160 | tf_op jit(solution)/shard_map/psum | solution.py:103
  860.6 165.7 %while.21 = (s32[]{:T(128)}, f32[8,128,256]{2,1,0:T(8,128)S(1)}, s32[]{:T(128)}, s32[256]{0:T(256)S(1)}, s32[]{:T(128)}, /*index=5*/bf16[256,128,128]{1,2,0:T(8,...) while((s32[]{:T(128)}, f32[8,128,256]{2,1,0:T(8,128)S(1)}, ...), condition=%wide.region_10.11_spmd, body=%wide.region_8.10_spmd.sunk | while | flops 135267456 | bytes 12063379 | solution.py:118
  864.3 3.2 convolution_select_fusion.5
  867.5 3.5 scatter_fusion.1
  877.9 3.5 scatter_fusion.1
  885.1 3.2 convolution_select_fusion.5
  888.2 3.5 scatter_fusion.1
  895.4 3.2 convolution_select_fusion.5
  898.6 3.5 scatter_fusion.1
  908.9 3.5 scatter_fusion.1
  919.3 3.5 scatter_fusion.1
  929.7 3.5 scatter_fusion.1
  936.8 3.2 convolution_select_fusion.5
  940.0 3.5 scatter_fusion.1
  950.4 3.5 scatter_fusion.1
  960.7 3.5 scatter_fusion.1
  971.1 3.5 scatter_fusion.1
  978.3 3.2 convolution_select_fusion.5
  981.5 3.5 scatter_fusion.1
  991.8 3.5 scatter_fusion.1
  1002.2 3.5 scatter_fusion.1
  1012.5 3.5 scatter_fusion.1
  1019.7 3.2 convolution_select_fusion.5
  1022.9 3.5 scatter_fusion.1
  (208 shorter events, 209.6 us)
Async XLA Ops:
  7.2 433.8 %copy-start = (bf16[1024,1024]{1,0:T(8,128)(2,1)S(1)}, bf16[1024,1024]{1,0:T(8,128)(2,1)}, u32[]{:S(2)}) copy-start(bf16[1024,1024]{1,0:T(8,128)(2,1)} %param.24) | copy-start | bytes 6291460
  7.2 280.7 %all-reduce.6.cloned.1.call-start = ((), (), s32[]{:S(2)}) async-start(), calls=%async_computation | async-start | bytes 1048576 | tf_op jit(solution)/shard_map/psum | solution.py:73
  9.3 3.9 copy-start.10
  9.3 3.9 copy-start.11
  181.6 259.4 %all-reduce.8.cloned.1.call-start = ((), (), s32[]{:S(2)}) async-start(), calls=%async_computation.1 | async-start | bytes 2097152 | tf_op jit(solution)/shard_map/psum | solution.py:81
  181.6 106.3 %copy-start.4 = (bf16[1,512,512]{2,1,0:T(8,128)(2,1)S(1)}, bf16[1,512,512]{2,1,0:T(8,128)(2,1)}, u32[]{:S(2)}) copy-start(bf16[1,512,512]{2,1,0:T(8,128)(2,1)} %param.23) | copy-start | bytes 1572868
  181.6 106.3 %copy-start.7 = (f32[1,512,256]{2,1,0:T(8,128)S(1)}, f32[1,512,256]{2,1,0:T(8,128)}, u32[]{:S(2)}) copy-start(f32[1,512,256]{2,1,0:T(8,128)} %param.19) | copy-start | bytes 1572868
  181.7 107.7 %copy-start.8 = (bf16[1,64,512]{2,1,0:T(8,128)(2,1)S(1)}, bf16[1,64,512]{2,1,0:T(8,128)(2,1)}, u32[]{:S(2)}) copy-start(bf16[1,64,512]{2,1,0:T(8,128)(2,1)} %param.30) | copy-start | bytes 196612
  294.0 299.2 %all-reduce.10.cloned.1.call-start = ((), (), s32[]{:S(2)}) async-start(), calls=%async_computation.2 | async-start | bytes 2097152 | tf_op jit(solution)/shard_map/psum | solution.py:90
  294.1 149.2 %copy-start.9 = (bf16[8,1024]{1,0:T(8,128)(2,1)S(1)}, bf16[8,1024]{1,0:T(8,128)(2,1)}, u32[]{:S(2)}) copy-start(bf16[8,1024]{1,0:T(8,128)(2,1)} %param.31) | copy-start | bytes 49156
  444.9 301.8 %all-reduce.12.cloned.1.call-start = ((), (), s32[]{:S(2)}) async-start(), calls=%async_computation.3 | async-start | bytes 2097152 | tf_op jit(solution)/shard_map/psum | solution.py:96
  598.3 151.2 %copy-start.1 = (bf16[1024,256]{0,1:T(8,128)(2,1)}, bf16[1024,256]{0,1:T(8,128)(2,1)S(1)}, u32[]{:S(2)}) copy-start(bf16[1024,256]{0,1:T(8,128)(2,1)S(1)} %get-tuple-element.162) | copy-start | bytes 1572868
  599.7 254.0 %all-reduce.14.cloned.1.call-start = ((), (), s32[]{:S(2)}) async-start(), calls=%async_computation.4 | async-start | bytes 524288 | tf_op jit(solution)/shard_map/psum | solution.py:103
  749.5 0.8 copy-start.2
  751.4 12.1 %copy-start.3 = (f32[1024,256]{0,1:T(8,128)S(1)}, f32[1024,256]{0,1:T(8,128)}, u32[]{:S(2)}) copy-start(f32[1024,256]{0,1:T(8,128)} %get-tuple-element.163) | copy-start | bytes 3145732
  764.8 89.0 %copy-start.5 = (bf16[1,512,512]{2,1,0:T(8,128)(2,1)S(1)}, bf16[1,512,512]{2,1,0:T(8,128)(2,1)}, u32[]{:S(2)}) copy-start(bf16[1,512,512]{2,1,0:T(8,128)(2,1)} %param.23) | copy-start | bytes 1572868
  860.6 165.8 %copy-start.6 = (bf16[1,8,128,128]{3,2,1,0:T(8,128)(2,1)S(1)}, bf16[1,8,128,128]{3,2,1,0:T(8,128)(2,1)}, u32[]{:S(2)}) copy-start(bf16[1,8,128,128]{3,2,1,0:T(8,128)(2,1)} %param.22) | copy-start | bytes 786436
Sparse Core Ops, SparseCore 0:
  181.7 106.1 all-reduce.5
  294.1 146.7 all-reduce.7
  446.4 146.7 all-reduce.9
  599.8 146.7 all-reduce.11
  751.5 102.1 all-reduce.13
where the time goes:
time: 1040 us
  waiting for transfers between devices  632 us (61%)
  other arithmetic  165 us (16%)
  matrix products  119 us (11%)
  local copies, waits for them, and re-layouts  103 us (10%)
  between operations  14.8 us (1%)
    psum x1, waiting for transfers between devices, solve_columns(): top_sum = lax.psum(top_part, ('leaf', 'grp'))  148 us
    psum x1, waiting for transfers between devices, solve_columns(): lax.psum(mid_terms, ('leaf', 'grp'))  147 us
    psum x1, waiting for transfers between devices, solve_columns(): mid_sum = lax.psum(upper[:MID_COLS], ('leaf', 'grp'))  147 us
    psum x1, waiting for transfers between devices, solve_columns(): group_sum = lax.psum(flat[:GROUP_COLS], 'grp')  103 us
    psum x1, waiting for transfers between devices, solve_columns(): lax.psum(group_terms.astype(jnp.bfloat16), 'grp').astype(jnp.float32)  86.4 us
    scatter-add x16, other arithmetic, forward_step(): return totals.at[target_block].add(terms)  83.2 us
    scatter-add x16, other arithmetic, backward_step(): return totals_back.at[column_block].add(terms)  55.9 us
    dot_general x16, matrix products, backward_step(): jnp.einsum('pji,pjr->pir', tile_block, picked, preferred_element_type=jnp...  51 us
  transfers between devices with their start and end apart: 5, of which 5 were waited for; matrix products, arithmetic and copies ran while one was open for 2% of the time, Pallas kernels for 0%

commit v1 on v0

v1 whole, which is shorter than its diff:
```python
import jax
import jax.numpy as jnp
from jax import lax
from jax.experimental import pallas as pl
from jax.experimental.pallas import tpu as pltpu
from jax.sharding import PartitionSpec as P

MESH = pl.DeviceIdType.MESH
BLOCK = 128
RHS = 256
LEAF_SN = 8
TILES = 256
UPPER = 2560
HALF = 1280
LEAF_ROWS = LEAF_SN * BLOCK
TILE_CHUNK = 16
F32 = jnp.float32
BF16 = jnp.bfloat16
ANY = pl.BlockSpec(memory_space=pl.ANY)
VMEM_IN = pl.BlockSpec(memory_space=pltpu.VMEM)
SMEM_IN = pl.BlockSpec(memory_space=pltpu.SMEM)
VMEM_LIMIT = 60 * 1024 * 1024

GROUP_SEG = (0, 256)
MID_SEG = (256, 512)
TOP_SEG = (768, 512)


def nn(a, b):
    return lax.dot_general(a, b, (((1,), (0,)), ((), ())), preferred_element_type=F32)


def nt(a, b):
    return lax.dot_general(a, b, (((1,), (1,)), ((), ())), preferred_element_type=F32)


def eye(n):
    rows = lax.broadcasted_iota(jnp.int32, (n, n), 0)
    cols = lax.broadcasted_iota(jnp.int32, (n, n), 1)
    return (rows == cols).astype(BF16)


def place_of(target):
    low = (target >> 1) * 10 + (target & 1)
    middle = ((target - 4) >> 2) * 10 + 2 + (target & 3)
    top = ((target - 12) >> 2) * 10 + 6 + (target & 3)
    return jnp.where(target < 4, low, jnp.where(target < 12, middle, top))


def build_kernel(col_s, tgt_s, cnt_s, tiles_h, inv, rhs, a_h, xt_out, tiles, dense32, dense, tsem, osem):
    count = cnt_s[0, 0]
    chunks = TILES // TILE_CHUNK

    def fetch(k):
        piece = pl.ds(k * TILE_CHUNK, TILE_CHUNK)
        return pltpu.make_async_copy(tiles_h.at[0, piece], tiles.at[piece], tsem.at[k])

    for k in range(chunks):
        @pl.when(k * TILE_CHUNK < count)
        def _():
            fetch(k).start()

    unit = eye(RHS)
    for s in range(LEAF_SN):
        rows = slice(s * BLOCK, (s + 1) * BLOCK)
        solved = nn(inv[0, s], rhs[0, rows, :].astype(BF16)).astype(BF16)
        xt_out[:, rows] = nt(unit, solved).astype(BF16)

    def clear(i, carry):
        for j in range(LEAF_SN):
            dense32[i * LEAF_SN + j] = jnp.zeros((BLOCK, BLOCK), F32)
        return carry

    lax.fori_loop(0, 20, clear, 0)

    def add_tile(p, carry):
        spot = place_of(tgt_s[0, p]) * LEAF_SN + col_s[0, p]
        dense32[spot] += tiles[p].astype(F32)
        return carry

    for k in range(chunks):
        @pl.when(k * TILE_CHUNK < count)
        def _():
            fetch(k).wait()
            lax.fori_loop(k * TILE_CHUNK, jnp.minimum(count, (k + 1) * TILE_CHUNK), add_tile, 0)

    def put(i):
        piece = pl.ds(i * 256, 256)
        return pltpu.make_async_copy(dense.at[piece], a_h.at[piece], osem.at[i])

    for i in range(10):
        for r in range(2):
            for s in range(LEAF_SN):
                block = 2 * i + r
                dense[block * BLOCK : (block + 1) * BLOCK, s * BLOCK : (s + 1) * BLOCK] = dense32[
                    block * LEAF_SN + s
                ].astype(BF16)
        put(i).start()
    for i in range(10):
        put(i).wait()


def upper_kernel(
    xt_h, a_h, rg_h, rm_h, rt_h, ig_h, im_h, it_h, gp_h, mp_h,
    out_h,
    xt, a, rg, rm, rt, ig, im, it, mp8, mpx, mpt, gpf, mpf,
    ps, prx, own, s_, yu, yd, yp, ym, sz, zu, zd, zp, zm,
    gres, xr, mres, tres, stage_t, stage_g, ab,
    lsem, ssem, rsem,
):
    x = lax.axis_index("leaf")
    g = lax.axis_index("grp")
    z = g // 8
    y = (g // 2) % 4
    c = g % 2

    def dev(xx, zz, yy, cc):
        return (xx % 4, (zz % 4) * 8 + (yy % 4) * 2 + cc)

    partner = dev(x, z, y, 1 - c)
    up = {"x": dev(x + 1, z, y, c), "y": dev(x, z, y + 1, c), "z": dev(x, z + 1, y, c)}
    down = {"x": dev(x + 3, z, y, c), "y": dev(x, z, y + 3, c), "z": dev(x, z + 3, y, c)}
    far_x = dev(x + 2, z, y, c)
    place = {"x": x, "y": y, "z": z}

    locals_ = []

    def fetch(src, dst):
        copy = pltpu.make_async_copy(src, dst, lsem.at[len(locals_)])
        locals_.append(copy)
        copy.start()
        return copy

    sent = []

    def send(src, dst, device):
        i = len(sent)
        copy = pltpu.make_async_remote_copy(
            src_ref=src, dst_ref=dst, send_sem=ssem.at[i], recv_sem=rsem.at[i],
            device_id=device, device_id_type=MESH,
        )
        sent.append(copy)
        copy.start()
        return copy

    def share(ref):
        return send(ref, ref, partner)

    own_gp = gpf.at[z, y, pl.ds(pl.multiple_of(c * 64, 64), 64), :]
    f_gp = fetch(gp_h.at[0], own_gp)
    f_mp = fetch(mp_h, mp8)
    f_xt = fetch(xt_h, xt)
    f_a = [fetch(a_h.at[1 - c, pl.ds(j * 256, 256)], a.at[j]) for j in range(5)]
    f_a += [fetch(a_h.at[c, pl.ds(j * 256, 256)], a.at[5 + j]) for j in range(5)]
    f_rg = fetch(rg_h.at[0, pl.ds(pl.multiple_of(c * 256, 256), 256)], rg)
    f_rm = fetch(rm_h.at[pl.ds(pl.multiple_of(c * 512, 512), 512)], rm)
    f_rt = fetch(rt_h.at[pl.ds(pl.multiple_of(c * 512, 512), 512)], rt)
    f_ig = fetch(ig_h.at[0], ig)
    f_im = fetch(im_h, im)
    f_it = fetch(it_h, it)

    peers = [partner, up["x"], down["x"], far_x, up["y"], down["y"], up["z"], down["z"]]
    barrier = pltpu.get_barrier_semaphore()
    for peer in peers:
        pl.semaphore_signal(barrier, inc=1, device_id=peer, device_id_type=MESH)
    pl.semaphore_wait(barrier, len(peers))

    class Ring:
        def __init__(self, axis, block, halves):
            self.axis, self.block, self.halves, self.me = axis, block, halves, place[axis]

        def start(self):
            mine = self.block(self.me)
            self.a = send(mine, mine, up[self.axis])
            self.b = send(mine, mine, down[self.axis])

        def relay(self):
            self.a.wait_recv()
            low = self.halves((self.me + 3) % 4)[0]
            self.c = send(low, low, up[self.axis])
            self.b.wait_recv()
            high = self.halves((self.me + 1) % 4)[1]
            self.d = send(high, high, down[self.axis])

        def finish(self):
            self.c.wait_recv()
            self.d.wait_recv()

    gp_rows = pl.ds(pl.multiple_of(c * 64, 64), 64)
    gp_y = Ring(
        "y",
        lambda i: gpf.at[z, i, gp_rows, :],
        lambda i: (gpf.at[z, i, gp_rows, 0:256], gpf.at[z, i, gp_rows, 256:512]),
    )
    gp_z = Ring(
        "z",
        lambda i: gpf.at[i, :, gp_rows, :],
        lambda i: (gpf.at[i, :, gp_rows, 0:256], gpf.at[i, :, gp_rows, 256:512]),
    )
    mp_z = Ring(
        "z",
        lambda i: mpf.at[c, x, i, y],
        lambda i: (mpf.at[c, x, i, y, :, 0:256], mpf.at[c, x, i, y, :, 256:512]),
    )
    mp_y = Ring(
        "y",
        lambda i: mpf.at[c, x, :, i],
        lambda i: (mpf.at[c, x, :, i, :, 0:256], mpf.at[c, x, :, i, :, 256:512]),
    )
    mp_x = Ring(
        "x",
        lambda i: mpf.at[c, i],
        lambda i: (mpf.at[c, i, :, :, :, 0:256], mpf.at[c, i, :, :, :, 256:512]),
    )

    f_gp.wait()
    gp_y.start()
    f_mp.wait()
    mpx[c] = mp8[...].astype(F32)
    m_pair = share(mpx.at[c])

    f_xt.wait()
    pair = []
    for j in range(5):
        f_a[j].wait()
        ps[j] = nt(xt[...], a[j]).astype(BF16)
        pair.append(send(ps.at[j], prx.at[j], partner))
        if j == 1:
            m_pair.wait_recv()
            both = jnp.concatenate([mpx[0], mpx[1]], axis=0).astype(BF16)
            mpt[0] = both[:, 0:512]
            mpt[1] = both[:, 512:1024]
            mpf[c, x, z, y] = mpt[c]
            mp_z.start()
    for j in range(5):
        f_a[5 + j].wait()
        own[j] = nt(xt[...], a[5 + j])

    def row(i, n):
        return pl.ds(pl.multiple_of((i % 4) * n, n), n)

    class Scatter:
        def __init__(self, axis, src, n, u, d, p, m, seg):
            self.axis, self.src, self.n, self.me = axis, src, n, place[axis]
            self.u, self.d, self.p, self.m = u, d, p, m
            o, width = seg
            h = width // 2
            self.low, self.high, self.all = slice(o, o + h), slice(o + h, o + width), slice(o, o + width)
            self.side = slice(o // 2, o // 2 + h)

        def start(self):
            me, n, src = self.me, self.n, self.src
            a_, b_ = up[self.axis], down[self.axis]
            self.c_u = send(src.at[row(me + 2, n), self.low], self.u.at[:, self.side], a_)
            self.c_d = send(src.at[row(me + 2, n), self.high], self.d.at[:, self.side], b_)
            self.c_p = send(src.at[row(me + 1, n), self.high], self.p.at[:, self.high], a_)
            self.c_m = send(src.at[row(me + 3, n), self.low], self.m.at[:, self.low], b_)

        def relay(self):
            me, n, src = self.me, self.n, self.src
            self.c_u.wait_recv()
            r = row(me + 1, n)
            src[r, self.low] = (src[r, self.low].astype(F32) + self.u[:, self.side].astype(F32)).astype(BF16)
            self.e_p = send(src.at[r, self.low], self.p.at[:, self.low], up[self.axis])
            self.c_d.wait_recv()
            r = row(me + 3, n)
            src[r, self.high] = (src[r, self.high].astype(F32) + self.d[:, self.side].astype(F32)).astype(BF16)
            self.e_m = send(src.at[r, self.high], self.m.at[:, self.high], down[self.axis])

        def finish(self):
            for copy in (self.c_p, self.c_m, self.e_p, self.e_m):
                copy.wait_recv()
            mine = self.src[row(self.me, self.n), self.all].astype(F32)
            return mine + self.p[:, self.all].astype(F32) + self.m[:, self.all].astype(F32)

    segments = (GROUP_SEG, MID_SEG, TOP_SEG)
    ry = [Scatter("y", s_, 64, yu, yd, yp, ym, seg) for seg in segments]
    rz = [Scatter("z", sz, 16, zu, zd, zp, zm, seg) for seg in segments]
    chunk_of = ((0,), (1, 2), (3, 4))

    for k in range(3):
        for j in chunk_of[k]:
            pair[j].wait_recv()
            s_[:, j * 256 : (j + 1) * 256] = (own[j] + prx[j].astype(F32)).astype(BF16)
        ry[k].start()
    gp_y.relay()
    mp_z.relay()
    ry[0].relay()
    gp_y.finish()
    gp_z.start()
    s_gp = [share(gp_z.block(z))]
    mp_z.finish()
    mp_y.start()
    ry[1].relay()
    ry[2].relay()

    first = y * 64 + z * 16
    pick = (
        lax.broadcasted_iota(jnp.int32, (16, RHS), 1)
        == lax.broadcasted_iota(jnp.int32, (16, RHS), 0) + first
    ).astype(BF16)

    def columns(ref):
        whole = ref[...]
        high = whole.astype(BF16)
        low = (whole - high.astype(F32)).astype(BF16)
        return nt(pick, high) + nt(pick, low)

    f_rg.wait()
    rg_t = columns(rg)
    f_rm.wait()
    rm_t = columns(rm)
    f_rt.wait()
    rt_t = columns(rt)

    for k in range(3):
        seg = segments[k]
        sz[:, seg[0] : seg[0] + seg[1]] = ry[k].finish().astype(BF16)
        rz[k].start()
    mp_y.relay()
    for k in range(3):
        rz[k].relay()
    mp_y.finish()
    mp_x.start()
    s_mp = [share(mp_x.block(x))]
    gp_z.relay()
    s_gp.append(share(gp_z.block((z + 3) % 4)))
    s_gp.append(share(gp_z.block((z + 1) % 4)))

    gres[c] = (rg_t - rz[0].finish()).astype(BF16)
    s_g = share(gres.at[c])
    mid_half = rz[1].finish()
    top_half = rz[2].finish()
    f_ig.wait()
    s_g.wait_recv()
    group_solved = nt(jnp.concatenate([gres[0], gres[1]], axis=1), ig[...]).astype(BF16)
    gp_z.finish()
    s_gp.append(share(gp_z.block((z + 2) % 4)))
    mp_x.relay()
    s_mp.append(share(mp_x.block((x + 3) % 4)))
    s_mp.append(share(mp_x.block((x + 1) % 4)))
    for copy in s_gp:
        copy.wait_recv()
    xr[x, 0] = (mid_half + nt(group_solved, gpf[c].reshape(512, 512))).astype(BF16)
    cross_m = [send(xr.at[x, 0], xr.at[x, 0], d) for d in (far_x, up["x"], down["x"])]
    xr[x, 1] = (top_half + nt(group_solved, gpf[2 + c].reshape(512, 512))).astype(BF16)
    cross_t = [send(xr.at[x, 1], xr.at[x, 1], d) for d in (far_x, up["x"], down["x"])]

    def total(k):
        return (
            (xr[0, k].astype(F32) + xr[1, k].astype(F32))
            + (xr[2, k].astype(F32) + xr[3, k].astype(F32))
        )

    for copy in cross_m:
        copy.wait_recv()
    mres[c] = (rm_t - total(0)).astype(BF16)
    s_m = share(mres.at[c])
    for copy in cross_t:
        copy.wait_recv()
    tres[c] = rt_t - total(1)
    s_t = share(tres.at[c])
    f_im.wait()
    s_m.wait_recv()
    mid_solved = nt(jnp.concatenate([mres[0], mres[1]], axis=1), im[...]).astype(BF16)
    mp_x.finish()
    s_mp.append(share(mp_x.block((x + 2) % 4)))
    for copy in s_mp:
        copy.wait_recv()
    below = nt(mid_solved[:, 0:512], mpf[0].reshape(1024, 512)) + nt(
        mid_solved[:, 512:1024], mpf[1].reshape(1024, 512)
    )
    s_t.wait_recv()
    f_it.wait()
    top_res = (jnp.concatenate([tres[0], tres[1]], axis=1) - below).astype(BF16)
    top_solved = nt(top_res, it[...]).astype(BF16)
    top_round = nn(top_solved, it[...]).astype(BF16)

    def gather(order, seg):
        lanes = slice(seg[0], seg[0] + seg[1])
        h = seg[1] // 2
        low, high = slice(seg[0], seg[0] + h), slice(seg[0] + h, seg[0] + seg[1])
        if order == "zy":
            return (
                Ring("z", lambda i: ab.at[c, y, i, :, lanes], lambda i: (ab.at[c, y, i, :, low], ab.at[c, y, i, :, high])),
                Ring("y", lambda i: ab.at[c, i, :, :, lanes], lambda i: (ab.at[c, i, :, :, low], ab.at[c, i, :, :, high])),
            )
        return (
            Ring("y", lambda i: ab.at[c, i, z, :, lanes], lambda i: (ab.at[c, i, z, :, low], ab.at[c, i, z, :, high])),
            Ring("z", lambda i: ab.at[c, :, i, :, lanes], lambda i: (ab.at[c, :, i, :, low], ab.at[c, :, i, :, high])),
        )

    rings = [gather("zy", TOP_SEG), gather("yz", MID_SEG), gather("zy", GROUP_SEG)]

    stage_t[0, 0] = top_round[:, 0:512]
    stage_t[0, 1] = top_round[:, 512:1024]
    ab[c, y, z, :, 768:1280] = stage_t[0, c]
    rings[0][0].start()

    mid_back = mid_solved.astype(F32) - jnp.concatenate(
        [nn(top_round, mpf[0].reshape(1024, 512)), nn(top_round, mpf[1].reshape(1024, 512))], axis=1
    )
    mid_round = nn(mid_back.astype(BF16), im[...]).astype(BF16)
    stage_t[1, 0] = mid_round[:, 0:512]
    stage_t[1, 1] = mid_round[:, 512:1024]
    ab[c, y, z, :, 256:768] = stage_t[1, c]
    rings[1][0].start()

    group_terms = (
        nn(mid_round[:, 0:512], gpf[0].reshape(512, 512))
        + nn(mid_round[:, 512:1024], gpf[1].reshape(512, 512))
        + nn(top_round[:, 0:512], gpf[2].reshape(512, 512))
        + nn(top_round[:, 512:1024], gpf[3].reshape(512, 512))
    )
    group_back = (group_solved.astype(F32) - group_terms).astype(BF16)
    group_round = nn(group_back, ig[...]).astype(BF16)
    stage_g[0] = group_round[:, 0:256]
    stage_g[1] = group_round[:, 256:512]
    ab[c, y, z, :, 0:256] = stage_g[c]
    rings[2][0].start()

    for first_ring, _ in rings:
        first_ring.relay()
    for first_ring, second_ring in rings:
        first_ring.finish()
        second_ring.start()
    last = []
    for _, second_ring in rings:
        last.append(share(second_ring.block(second_ring.me)))
    for _, second_ring in rings:
        second_ring.relay()
        last.append(share(second_ring.block((second_ring.me + 3) % 4)))
        last.append(share(second_ring.block((second_ring.me + 1) % 4)))
    for _, second_ring in rings:
        second_ring.finish()
        last.append(share(second_ring.block((second_ring.me + 2) % 4)))
    for copy in last:
        copy.wait_recv()
    fetch(ab, out_h).wait()
    for copy in sent:
        copy.wait_send()


def leaf_kernel(
    ab, a_h, xt, inv, leaf_h, group_h, mid_h, top_h,
    a, leaf_v, group_v, mid_v, top_v, asem, osem,
):
    def fetch(k):
        return pltpu.make_async_copy(a_h.at[k // 5, pl.ds((k % 5) * 256, 256)], a.at[k], asem.at[k])

    for k in range(10):
        fetch(k).start()

    outs = []

    def put(src, dst):
        copy = pltpu.make_async_copy(src, dst, osem.at[len(outs)])
        outs.append(copy)
        copy.start()

    unit = eye(RHS)

    def piece(k):
        lanes = slice((k % 5) * 256, (k % 5) * 256 + 256)
        return ab[k // 5, :, :, :, lanes].reshape(RHS, 256)

    for k in range(10):
        flipped = nt(unit, piece(k))
        h, j = k // 5, k % 5
        if j == 0:
            rows = pl.ds(h * 256, 256)
            group_v[rows, :] = flipped
            put(group_v.at[rows], group_h.at[0, rows])
        elif j < 3:
            rows = pl.ds(h * 512 + (j - 1) * 256, 256)
            mid_v[rows, :] = flipped
            put(mid_v.at[rows], mid_h.at[rows])
        else:
            rows = pl.ds(h * 512 + (j - 3) * 256, 256)
            top_v[rows, :] = flipped
            put(top_v.at[rows], top_h.at[rows])

    terms = None
    for k in range(10):
        fetch(k).wait()
        part = nn(piece(k), a[k])
        terms = part if terms is None else terms + part
    back = (xt[...].astype(F32) - terms).astype(BF16)
    small = eye(BLOCK)
    for s in range(LEAF_SN):
        rows = slice(s * BLOCK, (s + 1) * BLOCK)
        turned = nt(small, inv[0, s]).astype(BF16)
        leaf_v[rows, :] = nt(turned, back[:, rows])
        put(leaf_v.at[pl.ds(s * BLOCK, BLOCK)], leaf_h.at[0, pl.ds(s * BLOCK, BLOCK)])
    for copy in outs:
        copy.wait()


def body(
    rhs_leaf, rhs_group, rhs_middle, rhs_top, inv_leaf, inv_group, inv_middle, inv_top,
    leaf_tiles, tile_column, tile_target, tile_count, group_panel, middle_panel,
):
    shape = jax.ShapeDtypeStruct
    dense, xt = pl.pallas_call(
        build_kernel,
        name="build",
        out_shape=(shape((UPPER, LEAF_ROWS), BF16), shape((RHS, LEAF_ROWS), BF16)),
        in_specs=[SMEM_IN, SMEM_IN, SMEM_IN, ANY, VMEM_IN, VMEM_IN],
        out_specs=(ANY, VMEM_IN),
        scratch_shapes=[
            pltpu.VMEM((TILES, BLOCK, BLOCK), BF16),
            pltpu.VMEM((20 * LEAF_SN, BLOCK, BLOCK), F32),
            pltpu.VMEM((UPPER, LEAF_ROWS), BF16),
            pltpu.SemaphoreType.DMA((TILES // TILE_CHUNK,)),
            pltpu.SemaphoreType.DMA((10,)),
        ],
        compiler_params=pltpu.CompilerParams(vmem_limit_bytes=VMEM_LIMIT),
    )(tile_column, tile_target, tile_count, leaf_tiles, inv_leaf, rhs_leaf)
    dense = dense.reshape(2, HALF, LEAF_ROWS)
    vm = pltpu.VMEM
    above = pl.pallas_call(
        upper_kernel,
        name="upper",
        out_shape=shape((2, 4, 4, 16, HALF), BF16),
        in_specs=[ANY] * 10,
        out_specs=ANY,
        scratch_shapes=[
            vm((RHS, LEAF_ROWS), BF16),
            vm((10, 256, LEAF_ROWS), BF16),
            vm((256, RHS), F32),
            vm((512, RHS), F32),
            vm((512, RHS), F32),
            vm((512, 512), BF16),
            vm((1024, 1024), BF16),
            vm((1024, 1024), BF16),
            vm((8, 1024), BF16),
            vm((2, 8, 1024), F32),
            vm((2, 16, 512), BF16),
            vm((4, 4, 128, 512), BF16),
            vm((2, 4, 4, 4, 16, 512), BF16),
            vm((5, RHS, 256), BF16),
            vm((5, RHS, 256), BF16),
            vm((5, RHS, 256), F32),
            vm((RHS, HALF), BF16),
            vm((64, HALF // 2), BF16),
            vm((64, HALF // 2), BF16),
            vm((64, HALF), BF16),
            vm((64, HALF), BF16),
            vm((64, HALF), BF16),
            vm((16, HALF // 2), BF16),
            vm((16, HALF // 2), BF16),
            vm((16, HALF), BF16),
            vm((16, HALF), BF16),
            vm((2, 16, 256), BF16),
            vm((4, 2, 16, 512), BF16),
            vm((2, 16, 512), BF16),
            vm((2, 16, 512), F32),
            vm((2, 2, 16, 512), BF16),
            vm((2, 16, 256), BF16),
            vm((2, 4, 4, 16, HALF), BF16),
            pltpu.SemaphoreType.DMA((24,)),
            pltpu.SemaphoreType.DMA((128,)),
            pltpu.SemaphoreType.DMA((128,)),
        ],
        compiler_params=pltpu.CompilerParams(
            collective_id=0, has_side_effects=True, vmem_limit_bytes=VMEM_LIMIT
        ),
    )(xt, dense, rhs_group, rhs_middle, rhs_top, inv_group, inv_middle, inv_top, group_panel, middle_panel)
    return pl.pallas_call(
        leaf_kernel,
        name="leaf_back",
        out_shape=(
            shape((1, LEAF_ROWS, RHS), F32),
            shape((1, 512, RHS), F32),
            shape((1024, RHS), F32),
            shape((1024, RHS), F32),
        ),
        in_specs=[VMEM_IN, ANY, VMEM_IN, VMEM_IN],
        out_specs=(ANY, ANY, ANY, ANY),
        scratch_shapes=[
            vm((10, 256, LEAF_ROWS), BF16),
            vm((LEAF_ROWS, RHS), F32),
            vm((512, RHS), F32),
            vm((1024, RHS), F32),
            vm((1024, RHS), F32),
            pltpu.SemaphoreType.DMA((10,)),
            pltpu.SemaphoreType.DMA((18,)),
        ],
        compiler_params=pltpu.CompilerParams(vmem_limit_bytes=VMEM_LIMIT),
    )(above, dense, xt, inv_leaf)


def solution(mesh):
    placed = (
        P("leaf", "grp", None),
        P("leaf", None, None),
        P(),
        P(),
        P("leaf", "grp", None, None),
        P("leaf", None, None),
        P(),
        P(),
        P("leaf", "grp", None, None),
        P("leaf", "grp"),
        P("leaf", "grp"),
        P("leaf", "grp"),
        P("leaf", "grp", None),
        P(("leaf", "grp"), None),
    )
    return jax.shard_map(
        body,
        mesh=mesh,
        in_specs=placed,
        out_specs=(P("leaf", "grp", None), P("leaf", None, None), P(), P()),
        check_vma=False,
    )
```

time: 1040 us -> 81.7 us (0.08)
  the two profiles are of different devices: /device:TPU:4 before, /device:TPU:1 now
where the time goes in v1:
time: 81.7 us; the launch traced here: 81.4 us
  Pallas kernels  80.1 us (98%)
  between operations  1.29 us (2%)
    pallas_call x1, Pallas kernels, body(): pl.pallas_call(upper_kernel, name='upper', out_shape=shape((2, 4, 4, 16,...  64.7 us
    pallas_call x1, Pallas kernels, body(): pl.pallas_call(build_kernel, name='build', out_shape=(shape((UPPER, LEAF_...  8.42 us
    pallas_call x1, Pallas kernels, body(): pl.pallas_call(leaf_kernel, name='leaf_back', out_shape=(shape((1, LEAF_R...  6.95 us

profile of v1, /device:TPU:1, one launch (start us, length us, event | category | flops | bytes accessed | tf_op | source)
XLA Modules:
  0.0 81.4 jit_solution(17299865667449023742)
XLA Ops:
  1.3 8.4 %build.1 = (bf16[2560,1024]{1,0:T(8,128)(2,1)}, bf16[256,1024]{1,0:T(8,128)(2,1)}) custom-call(s32[1,256]{1,0:T(1,128)} %col_s.1, s32[1,256]{1,0:T(1,128)} %tgt_s.1, s32[1,1]{1,0:T(1,128)S(6)} %copy.18.cnt_s, bf16[1,256,128,128]{3,2,1,0:T(8,128)(2,1)} %tiles_h.1, bf16[1,8,128,128]{3,2,1,0:T(8,128)(2,1)} %inv.3, f32[1,1024,256]{2,1,0:T(8,128)} %rhs.1), custom_call_target="tpu_custom_call" | custom-call | tf_op jit(solution)/shard_map/build/pallas_call | solution.py:504
  9.7 64.7 %upper.1.ab = bf16[2,4,4,16,1280]{4,3,2,1,0:T(8,128)(2,1)} custom-call(bf16[256,1024]{1,0:T(8,128)(2,1)} %get-tuple-element.6.xt_h.xt, bf16[2,1280,1024]{2,1,0:T(8,128)(2,1)} %bitcast.1, f32[1,512,256]{2,1,0:T(8,128)} %rg_h.1, f32[1024,256]{1,0:T(8,128)} %rm_h.1, f32[1024,256]{1,0:T(8,128)} %rt_h.1, bf16[1,512,512]{2,1,0:T(8,128)(2,1)} %ig_h.1, ...), custom_call_target="tpu_custom_call" | custom-call | tf_op jit(solution)/shard_map/upper/pallas_call | solution.py:521
  74.4 7.0 %leaf_back.1 = (f32[1,1024,256]{2,1,0:T(8,128)}, f32[1,512,256]{2,1,0:T(8,128)}, f32[1024,256]{1,0:T(8,128)}, f32[1024,256]{1,0:T(8,128)}) custom-call(bf16[2,4,4,16,1280]{4,3,2,1,0:T(8,128)(2,1)} %upper.1.ab, bf16[2,1280,1024]{2,1,0:T(8,128)(2,1)} %bitcast.2, bf16[256,1024]{1,0:T(8,128)(2,1)} %get-tuple-element.6.xt_h.xt, bf16[1,8,128,128]{3,2,1,0:T(8,128)(2,1)} %inv.3), custom_call_target="tpu_custom_call" | custom-call | tf_op jit(solution)/shard_map/leaf_back/pallas_call | solution.py:569

commit v2 on v1

v2 whole, which is shorter than its diff:
```python
import jax
import jax.numpy as jnp
from jax import lax
from jax.experimental import pallas as pl
from jax.experimental.pallas import tpu as pltpu
from jax.sharding import PartitionSpec as P

MESH = pl.DeviceIdType.MESH
BLOCK = 128
RHS = 256
LEAF_SN = 8
TILES = 256
HALF = 1280
LEAF_ROWS = LEAF_SN * BLOCK
F32 = jnp.float32
BF16 = jnp.bfloat16
ANY = pl.BlockSpec(memory_space=pl.ANY)
VMEM_IN = pl.BlockSpec(memory_space=pltpu.VMEM)
SMEM_IN = pl.BlockSpec(memory_space=pltpu.SMEM)
VMEM_LIMIT = 60 * 1024 * 1024

GROUP_SEG = (0, 256)
MID_SEG = (256, 512)
TOP_SEG = (768, 512)


def nn(a, b):
    return lax.dot_general(a, b, (((1,), (0,)), ((), ())), preferred_element_type=F32)


def nt(a, b):
    return lax.dot_general(a, b, (((1,), (1,)), ((), ())), preferred_element_type=F32)


def eye(n):
    rows = lax.broadcasted_iota(jnp.int32, (n, n), 0)
    cols = lax.broadcasted_iota(jnp.int32, (n, n), 1)
    return (rows == cols).astype(BF16)


def place_of(target):
    low = (target >> 1) * 10 + (target & 1)
    middle = ((target - 4) >> 2) * 10 + 2 + (target & 3)
    top = ((target - 12) >> 2) * 10 + 6 + (target & 3)
    return jnp.where(target < 4, low, jnp.where(target < 12, middle, top))


def upper_kernel(
    col_v, tgt_v, cnt_s, rhs_h, inv_h, tiles_h, rg_h, rm_h, rt_h, ig_h, im_h, it_h, gp_h, mp_h,
    ab_h, back_h,
    rhs, inv, tiles, run, plan_v, plan_s, xt, a, rg, rm, rt, ig, im, it, mp8, mpx, mpt, gpf, mpf,
    ps, prx, own, s_, ya, zb, ta, tb, za, yb,
    gres, xr, stage_t, stage_g, ab, back,
    lsem, ssem, rsem,
):
    x = lax.axis_index("leaf")
    g = lax.axis_index("grp")
    z = g // 8
    y = (g // 2) % 4
    c = g % 2

    def dev(xx, zz, yy, cc):
        return (xx % 4, (zz % 4) * 8 + (yy % 4) * 2 + cc)

    partner = dev(x, z, y, 1 - c)
    on = {
        "x": [dev(x + d, z, y, c) for d in range(4)],
        "y": [dev(x, z, y + d, c) for d in range(4)],
        "z": [dev(x, z + d, y, c) for d in range(4)],
    }
    place = {"x": x, "y": y, "z": z}
    other_x = [dev(x + d, z, y, 1 - c) for d in range(4)]

    locals_ = []

    def fetch(src, dst):
        copy = pltpu.make_async_copy(src, dst, lsem.at[len(locals_)])
        locals_.append(copy)
        copy.start()
        return copy

    sent = []

    def send(src, dst, device):
        i = len(sent)
        copy = pltpu.make_async_remote_copy(
            src_ref=src, dst_ref=dst, send_sem=ssem.at[i], recv_sem=rsem.at[i],
            device_id=device, device_id_type=MESH,
        )
        sent.append(copy)
        copy.start()
        return copy

    def share(ref):
        return send(ref, ref, partner)

    peers = [partner] + on["x"][1:] + other_x[1:] + on["y"][1:] + on["z"][1:]
    barrier = pltpu.get_barrier_semaphore()
    for peer in peers:
        pl.semaphore_signal(barrier, inc=1, device_id=peer, device_id_type=MESH)

    gp_rows = pl.ds(pl.multiple_of(c * 64, 64), 64)
    f_gp = fetch(gp_h.at[0], gpf.at[z, y, gp_rows, :])
    f_mp = fetch(mp_h, mp8)
    f_inv = fetch(inv_h.at[0], inv)
    f_rhs = fetch(rhs_h.at[0], rhs)
    f_tiles = [fetch(tiles_h.at[0, pl.ds(i * 64, 64)], tiles.at[pl.ds(i * 64, 64)]) for i in range(4)]
    f_rg = fetch(rg_h.at[0, pl.ds(pl.multiple_of(c * 256, 256), 256)], rg)
    f_rm = fetch(rm_h, rm)
    f_rt = fetch(rt_h, rt)
    f_ig = fetch(ig_h.at[0], ig)
    f_im = fetch(im_h, im)
    f_it = fetch(it_h, it)

    count = cnt_s[0, 0]
    unit = eye(RHS)
    lane = lax.broadcasted_iota(jnp.int32, (1, TILES), 1)
    key = jnp.where(lane < count, place_of(tgt_v[...]) * LEAF_SN + col_v[...], 255).astype(F32)
    key_row = jnp.broadcast_to(key, (TILES, TILES))
    key_col = nt(unit, key_row.astype(BF16))
    ii = lax.broadcasted_iota(jnp.int32, (TILES, TILES), 0)
    jj = lax.broadcasted_iota(jnp.int32, (TILES, TILES), 1)
    ii_f, jj_f = ii.astype(F32), jj.astype(F32)

    def tally(mask, axis):
        return jnp.sum(jnp.where(mask, 1.0, 0.0), axis=axis, keepdims=True)

    rank = tally((key_row < key_col) | ((key_row == key_col) & (jj < ii)), 1)
    hit = rank == jj_f
    order = jnp.sum(jnp.where(hit, ii_f, 0.0), axis=0, keepdims=True)
    key_at = jnp.sum(jnp.where(hit, key_col, 0.0), axis=0, keepdims=True)
    key_before = jnp.sum(jnp.where(rank == jj_f - 1.0, key_col, 0.0), axis=0, keepdims=True)
    keep = jnp.where((key_at == key_before) & (lane > 0), 1.0, 0.0)
    up_to = tally(key_col <= jj_f, 0)
    last = jnp.where(up_to > tally(key_col < jj_f, 0), up_to - 1.0, 256.0)
    plan_v[0:1, :] = jnp.clip(order.astype(jnp.int32), 0, TILES - 1)
    plan_v[1:2, :] = keep.astype(jnp.int32)
    plan_v[2:3, :] = jnp.clip(last.astype(jnp.int32), 0, TILES)
    plan_v[3:8, :] = jnp.zeros((5, TILES), jnp.int32)
    f_plan = fetch(plan_v, plan_s)

    f_mp.wait()
    mpx[c] = mp8[...].astype(F32)

    f_inv.wait()
    f_rhs.wait()
    for s in range(LEAF_SN):
        rows = slice(s * BLOCK, (s + 1) * BLOCK)
        solved = nn(inv[s], rhs[rows, :].astype(BF16)).astype(BF16)
        xt[:, rows] = nt(unit, solved).astype(BF16)

    f_gp.wait()
    f_plan.wait()
    pl.semaphore_wait(barrier, len(peers))

    class Ring:
        def __init__(self, axis, block, halves):
            self.axis, self.block, self.halves, self.me = axis, block, halves, place[axis]

        def start(self):
            mine = self.block(self.me)
            self.a = send(mine, mine, on[self.axis][1])
            self.b = send(mine, mine, on[self.axis][3])

        def relay(self):
            self.a.wait_recv()
            low = self.halves((self.me + 3) % 4)[0]
            self.c = send(low, low, on[self.axis][1])
            self.b.wait_recv()
            high = self.halves((self.me + 1) % 4)[1]
            self.d = send(high, high, on[self.axis][3])

        def finish(self):
            self.c.wait_recv()
            self.d.wait_recv()

    class Direct:
        def __init__(self, axis, block):
            self.axis, self.block, self.me = axis, block, place[axis]

        def start(self):
            mine = self.block(self.me)
            self.copies = {d: send(mine, mine, on[self.axis][d]) for d in (2, 1, 3)}

        def finish(self):
            for d in (1, 3, 2):
                self.copies[d].wait_recv()

        def finish_and_share(self):
            out = [share(self.block(self.me))]
            for d in (1, 3, 2):
                self.copies[d].wait_recv()
                out.append(share(self.block((self.me + 4 - d) % 4)))
            return out

    gp_ay = Ring(
        "y",
        lambda i: gpf.at[z, i, gp_rows, 0:256],
        lambda i: (gpf.at[z, i, gp_rows, 0:128], gpf.at[z, i, gp_rows, 128:256]),
    )
    gp_az = Ring(
        "z",
        lambda i: gpf.at[i, :, gp_rows, 0:256],
        lambda i: (gpf.at[i, :, gp_rows, 0:128], gpf.at[i, :, gp_rows, 128:256]),
    )
    gp_bz = Ring(
        "z",
        lambda i: gpf.at[i, y, gp_rows, 256:512],
        lambda i: (gpf.at[i, y, gp_rows, 256:384], gpf.at[i, y, gp_rows, 384:512]),
    )
    gp_by = Ring(
        "y",
        lambda i: gpf.at[:, i, gp_rows, 256:512],
        lambda i: (gpf.at[:, i, gp_rows, 256:384], gpf.at[:, i, gp_rows, 384:512]),
    )
    mp_z = Direct("z", lambda i: mpf.at[c, x, i, y])
    mp_y = Direct("y", lambda i: mpf.at[c, x, :, i])
    mp_x = Ring(
        "x",
        lambda i: mpf.at[c, i],
        lambda i: (mpf.at[c, i, :, :, :, 0:256], mpf.at[c, i, :, :, :, 256:512]),
    )

    m_pair = share(mpx.at[c])
    gp_ay.start()
    gp_bz.start()

    for copy in f_tiles:
        copy.wait()

    def add_tile(p, total):
        total = total * plan_s[1, p].astype(F32) + tiles[plan_s[0, p]].astype(F32)
        run[p] = total.astype(BF16)
        return total

    def add_tiles(i, total):
        for q in range(4):
            total = add_tile(i * 4 + q, total)
        return total

    run[TILES] = jnp.zeros((BLOCK, BLOCK), BF16)
    total = lax.fori_loop(0, 16, add_tiles, jnp.zeros((BLOCK, BLOCK), F32))
    m_pair.wait_recv()
    both = jnp.concatenate([mpx[0], mpx[1]], axis=0).astype(BF16)
    mpt[0] = both[:, 0:512]
    mpt[1] = both[:, 512:1024]
    mpf[c, x, z, y] = mpt[c]
    mp_z.start()
    total = lax.fori_loop(16, 32, add_tiles, total)
    gp_ay.relay()
    gp_bz.relay()
    total = lax.fori_loop(32, 48, add_tiles, total)
    mp_z.finish()
    mp_y.start()
    total = lax.fori_loop(48, 64, add_tiles, total)
    gp_ay.finish()
    gp_az.start()
    gp_bz.finish()
    gp_by.start()

    def assemble(chunk):
        for r in range(2):
            for s in range(LEAF_SN):
                a[chunk, r * BLOCK : (r + 1) * BLOCK, s * BLOCK : (s + 1) * BLOCK] = run[
                    plan_s[2, (chunk * 2 + r) * LEAF_SN + s]
                ]

    pair = []
    for j in range(5):
        chunk = (1 - c) * 5 + j
        assemble(chunk)
        ps[j] = nt(xt[...], a[chunk]).astype(BF16)
        pair.append(send(ps.at[j], prx.at[j], partner))
    mp_y.finish()
    mp_x.start()
    for j in range(5):
        chunk = c * 5 + j
        assemble(chunk)
        own[j] = nt(xt[...], a[chunk])

    class Scatter:
        def __init__(self, seg):
            o, width = seg
            h = width // 2
            self.low, self.high = slice(o, o + h), slice(o + h, o + width)
            self.side = slice(o // 2, o // 2 + h)

        def first(self):
            side = self.side
            self.y1 = [
                send(s_.at[(y + d) % 4, :, :, self.low], ya.at[d - 1, :, :, side], on["y"][d]) for d in (2, 1, 3)
            ]
            self.z1 = [
                send(s_.at[:, (z + d) % 4, :, self.high], zb.at[d - 1, :, :, side], on["z"][d]) for d in (2, 1, 3)
            ]

        def second(self):
            side = self.side
            for copy in self.y1:
                copy.wait_recv()
            total = s_[y, :, :, self.low].astype(F32)
            for d in range(3):
                total += ya[d, :, :, side].astype(F32)
            ta[:, :, side] = total.astype(BF16)
            self.z2 = [send(ta.at[(z + d) % 4, :, side], za.at[d - 1, :, side], on["z"][d]) for d in (2, 1, 3)]
            for copy in self.z1:
                copy.wait_recv()
            total = s_[:, z, :, self.high].astype(F32)
            for d in range(3):
                total += zb[d, :, :, side].astype(F32)
            tb[:, :, side] = total.astype(BF16)
            self.y2 = [send(tb.at[(y + d) % 4, :, side], yb.at[d - 1, :, side], on["y"][d]) for d in (2, 1, 3)]

        def finish(self):
            side = self.side
            for copy in self.z2 + self.y2:
                copy.wait_recv()
            low, high = ta[z, :, side].astype(F32), tb[y, :, side].astype(F32)
            for d in range(3):
                low += za[d, :, side].astype(F32)
                high += yb[d, :, side].astype(F32)
            return jnp.concatenate([low, high], axis=1)

    scatters = [Scatter(seg) for seg in (GROUP_SEG, MID_SEG, TOP_SEG)]
    chunk_of = ((0,), (1, 2), (3, 4))
    for k in range(3):
        for j in chunk_of[k]:
            pair[j].wait_recv()
            s_[:, :, :, j * 256 : (j + 1) * 256] = (
                (own[j] + prx[j].astype(F32)).astype(BF16).reshape(4, 4, 16, 256)
            )
        scatters[k].first()

    first = y * 64 + z * 16
    pick = (
        lax.broadcasted_iota(jnp.int32, (16, RHS), 1)
        == lax.broadcasted_iota(jnp.int32, (16, RHS), 0) + first
    ).astype(BF16)

    def columns(ref):
        whole = ref[...]
        high = whole.astype(BF16)
        low = (whole - high.astype(F32)).astype(BF16)
        return nt(pick, high) + nt(pick, low)

    f_rg.wait()
    rg_t = columns(rg)
    f_rm.wait()
    rm_t = columns(rm)
    f_rt.wait()
    rt_t = columns(rt)

    for scatter in scatters:
        scatter.second()
    gp_az.relay()
    gp_by.relay()
    s_gp = []
    for ring in (gp_az, gp_by):
        for d in (0, 3, 1):
            s_gp.append(share(ring.block((ring.me + d) % 4)))
    mp_x.relay()
    s_mp = [share(mp_x.block((x + d) % 4)) for d in (0, 3, 1)]

    gres[c] = (rg_t - scatters[0].finish()).astype(BF16)
    s_g = share(gres.at[c])
    mid_half = scatters[1].finish()
    top_half = scatters[2].finish()
    f_ig.wait()
    s_g.wait_recv()
    group_solved = nt(jnp.concatenate([gres[0], gres[1]], axis=1), ig[...]).astype(BF16)
    for ring in (gp_az, gp_by):
        ring.finish()
        s_gp.append(share(ring.block((ring.me + 2) % 4)))
    for copy in s_gp:
        copy.wait_recv()

    def cross(k, half, panel):
        xr[x, k, c] = (half + nt(group_solved, gpf[panel].reshape(512, 512))).astype(BF16)
        mine = xr.at[x, k, c]
        to = [on["x"][2], other_x[2], on["x"][1], other_x[1], on["x"][3], other_x[3], partner]
        return [send(mine, mine, device) for device in to]

    def total_of(k):
        halves = []
        for h in range(2):
            halves.append(
                (xr[0, k, h].astype(F32) + xr[1, k, h].astype(F32))
                + (xr[2, k, h].astype(F32) + xr[3, k, h].astype(F32))
            )
        return jnp.concatenate(halves, axis=1)

    cross_m = cross(0, mid_half, c)
    cross_t = cross(1, top_half, 2 + c)
    f_im.wait()
    for copy in cross_m:
        copy.wait_recv()
    mid_solved = nt((rm_t - total_of(0)).astype(BF16), im[...]).astype(BF16)
    mp_x.finish()
    s_mp.append(share(mp_x.block((x + 2) % 4)))
    for copy in s_mp:
        copy.wait_recv()
    below = nt(mid_solved[:, 0:512], mpf[0].reshape(1024, 512)) + nt(
        mid_solved[:, 512:1024], mpf[1].reshape(1024, 512)
    )
    f_it.wait()
    for copy in cross_t:
        copy.wait_recv()
    top_solved = nt((rt_t - total_of(1) - below).astype(BF16), it[...]).astype(BF16)
    top_round = nn(top_solved, it[...]).astype(BF16)

    class Gather:
        def __init__(self, seg):
            o, width = seg
            h = width // 2
            low, high = slice(o, o + h), slice(o + h, o + width)
            self.lanes = slice(o, o + width)
            self.z1 = Direct("z", lambda i: ab.at[c, y, i, :, low])
            self.y1 = Direct("y", lambda i: ab.at[c, i, z, :, high])
            self.y2 = Direct("y", lambda i: ab.at[c, i, :, :, low])
            self.z2 = Direct("z", lambda i: ab.at[c, :, i, :, high])

        def first(self, value):
            ab[c, y, z, :, self.lanes] = value
            self.z1.start()
            self.y1.start()

        def second(self):
            self.z1.finish()
            self.y2.start()
            self.y1.finish()
            self.z2.start()

        def finish(self):
            self.shares = self.y2.finish_and_share() + self.z2.finish_and_share()

        def arrive(self):
            for copy in self.shares:
                copy.wait_recv()

    gathers = [Gather(seg) for seg in (GROUP_SEG, MID_SEG, TOP_SEG)]
    stage_t[0, 0] = top_round[:, 0:512]
    stage_t[0, 1] = top_round[:, 512:1024]
    gathers[2].first(stage_t[0, c])

    mid_back = mid_solved.astype(F32) - jnp.concatenate(
        [nn(top_round, mpf[0].reshape(1024, 512)), nn(top_round, mpf[1].reshape(1024, 512))], axis=1
    )
    mid_round = nn(mid_back.astype(BF16), im[...]).astype(BF16)
    stage_t[1, 0] = mid_round[:, 0:512]
    stage_t[1, 1] = mid_round[:, 512:1024]
    gathers[1].first(stage_t[1, c])

    group_terms = (
        nn(mid_round[:, 0:512], gpf[0].reshape(512, 512))
        + nn(mid_round[:, 512:1024], gpf[1].reshape(512, 512))
        + nn(top_round[:, 0:512], gpf[2].reshape(512, 512))
        + nn(top_round[:, 512:1024], gpf[3].reshape(512, 512))
    )
    group_back = (group_solved.astype(F32) - group_terms).astype(BF16)
    group_round = nn(group_back, ig[...]).astype(BF16)
    stage_g[0] = group_round[:, 0:256]
    stage_g[1] = group_round[:, 256:512]
    gathers[0].first(stage_g[c])

    gathers[2].second()
    gathers[1].second()
    gathers[0].second()

    def product(k):
        terms = None
        for h in range(2):
            for j in chunk_of[k]:
                part = nn(ab[h, :, :, :, j * 256 : (j + 1) * 256].reshape(RHS, 256), a[h * 5 + j])
                terms = part if terms is None else terms + part
        return terms

    rest = xt[...].astype(F32)
    for k in (2, 1, 0):
        gathers[k].finish()
        gathers[k].arrive()
        rest = rest - product(k)
    back[...] = rest.astype(BF16)
    f_out = fetch(ab, ab_h)
    f_back = fetch(back, back_h)
    f_out.wait()
    f_back.wait()
    for copy in sent:
        copy.wait_send()


def leaf_kernel(ab, back, inv, leaf_h, group_h, mid_h, top_h, leaf_v, group_v, mid_v, top_v, osem):
    outs = []

    def put(src, dst):
        copy = pltpu.make_async_copy(src, dst, osem.at[len(outs)])
        outs.append(copy)
        copy.start()

    unit = eye(RHS)
    for k in range(10):
        h, j = k // 5, k % 5
        flipped = nt(unit, ab[h, :, :, :, j * 256 : (j + 1) * 256].reshape(RHS, 256))
        if j == 0:
            rows = pl.ds(h * 256, 256)
            group_v[rows, :] = flipped
            put(group_v.at[rows], group_h.at[0, rows])
        elif j < 3:
            rows = pl.ds(h * 512 + (j - 1) * 256, 256)
            mid_v[rows, :] = flipped
            put(mid_v.at[rows], mid_h.at[rows])
        else:
            rows = pl.ds(h * 512 + (j - 3) * 256, 256)
            top_v[rows, :] = flipped
            put(top_v.at[rows], top_h.at[rows])
    small = eye(BLOCK)
    for s in range(LEAF_SN):
        rows = slice(s * BLOCK, (s + 1) * BLOCK)
        turned = nt(small, inv[0, s]).astype(BF16)
        leaf_v[rows, :] = nt(turned, back[:, rows])
        put(leaf_v.at[pl.ds(s * BLOCK, BLOCK)], leaf_h.at[0, pl.ds(s * BLOCK, BLOCK)])
    for copy in outs:
        copy.wait()


def body(
    rhs_leaf, rhs_group, rhs_middle, rhs_top, inv_leaf, inv_group, inv_middle, inv_top,
    leaf_tiles, tile_column, tile_target, tile_count, group_panel, middle_panel,
):
    shape = jax.ShapeDtypeStruct
    vm = pltpu.VMEM
    above, back = pl.pallas_call(
        upper_kernel,
        name="upper",
        out_shape=(shape((2, 4, 4, 16, HALF), BF16), shape((RHS, LEAF_ROWS), BF16)),
        in_specs=[VMEM_IN, VMEM_IN, SMEM_IN] + [ANY] * 11,
        out_specs=(ANY, ANY),
        scratch_shapes=[
            vm((LEAF_ROWS, RHS), F32),
            vm((LEAF_SN, BLOCK, BLOCK), BF16),
            vm((TILES, BLOCK, BLOCK), BF16),
            vm((TILES + 1, BLOCK, BLOCK), BF16),
            vm((8, TILES), jnp.int32),
            pltpu.SMEM((8, TILES), jnp.int32),
            vm((RHS, LEAF_ROWS), BF16),
            vm((10, 256, LEAF_ROWS), BF16),
            vm((256, RHS), F32),
            vm((1024, RHS), F32),
            vm((1024, RHS), F32),
            vm((512, 512), BF16),
            vm((1024, 1024), BF16),
            vm((1024, 1024), BF16),
            vm((8, 1024), BF16),
            vm((2, 8, 1024), F32),
            vm((2, 16, 512), BF16),
            vm((4, 4, 128, 512), BF16),
            vm((2, 4, 4, 4, 16, 512), BF16),
            vm((5, RHS, 256), BF16),
            vm((5, RHS, 256), BF16),
            vm((5, RHS, 256), F32),
            vm((4, 4, 16, HALF), BF16),
            vm((3, 4, 16, HALF // 2), BF16),
            vm((3, 4, 16, HALF // 2), BF16),
            vm((4, 16, HALF // 2), BF16),
            vm((4, 16, HALF // 2), BF16),
            vm((3, 16, HALF // 2), BF16),
            vm((3, 16, HALF // 2), BF16),
            vm((2, 16, 256), BF16),
            vm((4, 2, 2, 16, 512), BF16),
            vm((2, 2, 16, 512), BF16),
            vm((2, 16, 256), BF16),
            vm((2, 4, 4, 16, HALF), BF16),
            vm((RHS, LEAF_ROWS), BF16),
            pltpu.SemaphoreType.DMA((24,)),
            pltpu.SemaphoreType.DMA((180,)),
            pltpu.SemaphoreType.DMA((180,)),
        ],
        compiler_params=pltpu.CompilerParams(
            collective_id=0, has_side_effects=True, vmem_limit_bytes=VMEM_LIMIT
        ),
    )(
        tile_column, tile_target, tile_count, rhs_leaf, inv_leaf, leaf_tiles,
        rhs_group, rhs_middle, rhs_top, inv_group, inv_middle, inv_top, group_panel, middle_panel,
    )
    return pl.pallas_call(
        leaf_kernel,
        name="leaf_back",
        out_shape=(
            shape((1, LEAF_ROWS, RHS), F32),
            shape((1, 512, RHS), F32),
            shape((1024, RHS), F32),
            shape((1024, RHS), F32),
        ),
        in_specs=[VMEM_IN, VMEM_IN, VMEM_IN],
        out_specs=(ANY, ANY, ANY, ANY),
        scratch_shapes=[
            vm((LEAF_ROWS, RHS), F32),
            vm((512, RHS), F32),
            vm((1024, RHS), F32),
            vm((1024, RHS), F32),
            pltpu.SemaphoreType.DMA((18,)),
        ],
        compiler_params=pltpu.CompilerParams(vmem_limit_bytes=VMEM_LIMIT),
    )(above, back, inv_leaf)


def solution(mesh):
    placed = (
        P("leaf", "grp", None),
        P("leaf", None, None),
        P(),
        P(),
        P("leaf", "grp", None, None),
        P("leaf", None, None),
        P(),
        P(),
        P("leaf", "grp", None, None),
        P("leaf", "grp"),
        P("leaf", "grp"),
        P("leaf", "grp"),
        P("leaf", "grp", None),
        P(("leaf", "grp"), None),
    )
    return jax.shard_map(
        body,
        mesh=mesh,
        in_specs=placed,
        out_specs=(P("leaf", "grp", None), P("leaf", None, None), P(), P()),
        check_vma=False,
    )
```

time: 81.7 us -> 64.1 us (0.78)
  Pallas kernels: 80.1 us -> 62.6 us
    pallas_call x2 -> x1, Pallas kernels: 73.1 us -> 58.9 us  [body(): pl.pallas_call(upper_kernel, name='upper', out_shape=(shape((2, 4, 4, 16,...]
    pallas_call x1, Pallas kernels: 6.95 us -> 3.74 us  [body(): pl.pallas_call(leaf_kernel, name='leaf_back', out_shape=(shape((1, LEAF_R...]
where the time goes in v2:
time: 64.1 us; the launch traced here: 63.9 us
  Pallas kernels  62.6 us (98%)
  between operations  1.29 us (2%)
    pallas_call x1, Pallas kernels, body(): pl.pallas_call(upper_kernel, name='upper', out_shape=(shape((2, 4, 4, 16,...  58.9 us
    pallas_call x1, Pallas kernels, body(): pl.pallas_call(leaf_kernel, name='leaf_back', out_shape=(shape((1, LEAF_R...  3.74 us

profile of v2, /device:TPU:1, one launch (start us, length us, event | category | flops | bytes accessed | tf_op | source)
XLA Modules:
  0.0 63.9 jit_solution(14643386343902595297)
XLA Ops:
  1.3 58.9 %upper.1 = (bf16[2,4,4,16,1280]{4,3,2,1,0:T(8,128)(2,1)}, bf16[256,1024]{1,0:T(8,128)(2,1)}) custom-call(s32[1,256]{1,0:T(1,128)} %col_v.1, s32[1,256]{1,0:T(1,128)} %tgt_v.1, s32[1,1]{1,0:T(1,128)S(6)} %copy.18.cnt_s, f32[1,1024,256]{2,1,0:T(8,128)} %rhs_h.1, bf16[1,8,128,128]{3,2,1,0:T(8,128)(2,1)} %inv.1, bf16[1,256,128,128]{3,2,1,0:T(8,128)(2,1)} %tiles_h.1, ...), custom_call_target="tpu_custom_call" | custom-call | tf_op jit(solution)/shard_map/upper/pallas_call | solution.py:531
  60.1 3.7 %leaf_back.1 = (f32[1,1024,256]{2,1,0:T(8,128)}, f32[1,512,256]{2,1,0:T(8,128)}, f32[1024,256]{1,0:T(8,128)}, f32[1024,256]{1,0:T(8,128)}) custom-call(bf16[2,4,4,16,1280]{4,3,2,1,0:T(8,128)(2,1)} %get-tuple-element.6.ab, bf16[256,1024]{1,0:T(8,128)(2,1)} %get-tuple-element.7.back, bf16[1,8,128,128]{3,2,1,0:T(8,128)(2,1)} %inv.1), custom_call_target="tpu_custom_call" | custom-call | tf_op jit(solution)/shard_map/leaf_back/pallas_call | solution.py:584

commit v3 on v2

--- a/solution.py
+++ b/solution.py
@@ -48,8 +48,8 @@
 def upper_kernel(
     col_v, tgt_v, cnt_s, rhs_h, inv_h, tiles_h, rg_h, rm_h, rt_h, ig_h, im_h, it_h, gp_h, mp_h,
     ab_h, back_h,
-    rhs, inv, tiles, run, plan_v, plan_s, xt, a, rg, rm, rt, ig, im, it, mp8, mpx, mpt, gpf, mpf,
-    ps, prx, own, s_, ya, zb, ta, tb, za, yb,
+    rhs, inv, tiles, run, plan_v, plan_s, xt, rg, rm, rt, ig, im, it, mp8, mpx, mpt, gpf, mpf,
+    ps, prx, s_, ya, zb, ta, tb, za, yb,
     gres, xr, stage_t, stage_g, ab, back,
     lsem, ssem, rsem,
 ):
@@ -94,7 +94,8 @@
     def share(ref):
         return send(ref, ref, partner)
 
-    peers = [partner] + on["x"][1:] + other_x[1:] + on["y"][1:] + on["z"][1:]
+    plane = [dev(x, z + dz, y + dy, c) for dz in (2, 1, 3, 0) for dy in (2, 1, 3, 0) if dz or dy]
+    peers = [partner] + on["x"][1:] + other_x[1:] + plane
     barrier = pltpu.get_barrier_semaphore()
     for peer in peers:
         pl.semaphore_signal(barrier, inc=1, device_id=peer, device_id_type=MESH)
@@ -105,12 +106,6 @@
     f_inv = fetch(inv_h.at[0], inv)
     f_rhs = fetch(rhs_h.at[0], rhs)
     f_tiles = [fetch(tiles_h.at[0, pl.ds(i * 64, 64)], tiles.at[pl.ds(i * 64, 64)]) for i in range(4)]
-    f_rg = fetch(rg_h.at[0, pl.ds(pl.multiple_of(c * 256, 256), 256)], rg)
-    f_rm = fetch(rm_h, rm)
-    f_rt = fetch(rt_h, rt)
-    f_ig = fetch(ig_h.at[0], ig)
-    f_im = fetch(im_h, im)
-    f_it = fetch(it_h, it)
 
     count = cnt_s[0, 0]
     unit = eye(RHS)
@@ -227,6 +222,13 @@
 
     for copy in f_tiles:
         copy.wait()
+    side = pl.ds(pl.multiple_of((y // 2) * 128, 128), 128)
+    f_rg = fetch(rg_h.at[0, pl.ds(pl.multiple_of(c * 256, 256), 256), side], rg)
+    f_rm = fetch(rm_h.at[:, side], rm)
+    f_rt = fetch(rt_h.at[:, side], rt)
+    f_ig = fetch(ig_h.at[0], ig)
+    f_im = fetch(im_h, im)
+    f_it = fetch(it_h, it)
 
     def add_tile(p, total):
         total = total * plan_s[1, p].astype(F32) + tiles[plan_s[0, p]].astype(F32)
@@ -258,25 +260,12 @@
     gp_bz.finish()
     gp_by.start()
 
-    def assemble(chunk):
+    def dense(chunk):
+        rows = []
         for r in range(2):
-            for s in range(LEAF_SN):
-                a[chunk, r * BLOCK : (r + 1) * BLOCK, s * BLOCK : (s + 1) * BLOCK] = run[
-                    plan_s[2, (chunk * 2 + r) * LEAF_SN + s]
-                ]
-
-    pair = []
-    for j in range(5):
-        chunk = (1 - c) * 5 + j
-        assemble(chunk)
-        ps[j] = nt(xt[...], a[chunk]).astype(BF16)
-        pair.append(send(ps.at[j], prx.at[j], partner))
-    mp_y.finish()
-    mp_x.start()
-    for j in range(5):
-        chunk = c * 5 + j
-        assemble(chunk)
-        own[j] = nt(xt[...], a[chunk])
+            spots = [plan_s[2, (chunk * 2 + r) * LEAF_SN + s] for s in range(LEAF_SN)]
+            rows.append(jnp.concatenate([run[spot] for spot in spots], axis=1))
+        return jnp.concatenate(rows, axis=0)
 
     class Scatter:
         def __init__(self, seg):
@@ -323,18 +312,38 @@
 
     scatters = [Scatter(seg) for seg in (GROUP_SEG, MID_SEG, TOP_SEG)]
     chunk_of = ((0,), (1, 2), (3, 4))
-    for k in range(3):
-        for j in chunk_of[k]:
-            pair[j].wait_recv()
-            s_[:, :, :, j * 256 : (j + 1) * 256] = (
-                (own[j] + prx[j].astype(F32)).astype(BF16).reshape(4, 4, 16, 256)
-            )
-        scatters[k].first()
-
-    first = y * 64 + z * 16
+    pair = {}
+
+    def give(j):
+        ps[j] = nt(xt[...], dense((1 - c) * 5 + j)).astype(BF16)
+        pair[j] = send(ps.at[j], prx.at[j], partner)
+
+    def take(j):
+        mine = nt(xt[...], dense(c * 5 + j))
+        pair[j].wait_recv()
+        s_[:, :, :, j * 256 : (j + 1) * 256] = (
+            (mine + prx[j].astype(F32)).astype(BF16).reshape(4, 4, 16, 256)
+        )
+
+    for j in range(3):
+        give(j)
+    take(0)
+    scatters[0].first()
+    give(3)
+    give(4)
+    take(1)
+    take(2)
+    scatters[1].first()
+    mp_y.finish()
+    mp_x.start()
+    take(3)
+    take(4)
+    scatters[2].first()
+
+    first = (y % 2) * 64 + z * 16
     pick = (
-        lax.broadcasted_iota(jnp.int32, (16, RHS), 1)
-        == lax.broadcasted_iota(jnp.int32, (16, RHS), 0) + first
+        lax.broadcasted_iota(jnp.int32, (16, 128), 1)
+        == lax.broadcasted_iota(jnp.int32, (16, 128), 0) + first
     ).astype(BF16)
 
     def columns(ref):
@@ -437,7 +446,25 @@
             for copy in self.shares:
                 copy.wait_recv()
 
-    gathers = [Gather(seg) for seg in (GROUP_SEG, MID_SEG, TOP_SEG)]
+    class GatherOnce:
+        def first(self, value):
+            ab[c, y, z, :, 0:256] = value
+            mine = ab.at[c, y, z, :, 0:256]
+            self.copies = [send(mine, mine, device) for device in plane]
+
+        def second(self):
+            pass
+
+        def finish(self):
+            for copy in self.copies:
+                copy.wait_recv()
+            self.shares = [share(ab.at[c, :, :, :, 0:256])]
+
+        def arrive(self):
+            for copy in self.shares:
+                copy.wait_recv()
+
+    gathers = [GatherOnce(), Gather(MID_SEG), Gather(TOP_SEG)]
     stage_t[0, 0] = top_round[:, 0:512]
     stage_t[0, 1] = top_round[:, 512:1024]
     gathers[2].first(stage_t[0, c])
@@ -467,23 +494,29 @@
     gathers[0].second()
 
     def product(k):
-        terms = None
-        for h in range(2):
-            for j in chunk_of[k]:
-                part = nn(ab[h, :, :, :, j * 256 : (j + 1) * 256].reshape(RHS, 256), a[h * 5 + j])
-                terms = part if terms is None else terms + part
-        return terms
+        pieces = [(h, j) for h in range(2) for j in chunk_of[k]]
+        left = [ab[h, :, :, :, j * 256 : (j + 1) * 256].reshape(RHS, 256) for h, j in pieces]
+        right = [dense(h * 5 + j) for h, j in pieces]
+        return nn(jnp.concatenate(left, axis=1), jnp.concatenate(right, axis=0))
 
     rest = xt[...].astype(F32)
-    for k in (2, 1, 0):
-        gathers[k].finish()
+    out = []
+    def settle(k):
         gathers[k].arrive()
-        rest = rest - product(k)
+        lanes = slice(chunk_of[k][0] * 256, chunk_of[k][-1] * 256 + 256)
+        out.append(fetch(ab.at[:, :, :, :, lanes], ab_h.at[:, :, :, :, lanes]))
+        return rest - product(k)
+
+    gathers[0].finish()
+    gathers[2].finish()
+    rest = settle(0)
+    gathers[1].finish()
+    rest = settle(2)
+    rest = settle(1)
     back[...] = rest.astype(BF16)
-    f_out = fetch(ab, ab_h)
-    f_back = fetch(back, back_h)
-    f_out.wait()
-    f_back.wait()
+    out.append(fetch(back, back_h))
+    for copy in out:
+        copy.wait()
     for copy in sent:
         copy.wait_send()
 
@@ -542,10 +575,9 @@
             vm((8, TILES), jnp.int32),
             pltpu.SMEM((8, TILES), jnp.int32),
             vm((RHS, LEAF_ROWS), BF16),
-            vm((10, 256, LEAF_ROWS), BF16),
-            vm((256, RHS), F32),
-            vm((1024, RHS), F32),
-            vm((1024, RHS), F32),
+            vm((256, 128), F32),
+            vm((1024, 128), F32),
+            vm((1024, 128), F32),
             vm((512, 512), BF16),
             vm((1024, 1024), BF16),
             vm((1024, 1024), BF16),
@@ -556,7 +588,6 @@
             vm((2, 4, 4, 4, 16, 512), BF16),
             vm((5, RHS, 256), BF16),
             vm((5, RHS, 256), BF16),
-            vm((5, RHS, 256), F32),
             vm((4, 4, 16, HALF), BF16),
             vm((3, 4, 16, HALF // 2), BF16),
             vm((3, 4, 16, HALF // 2), BF16),

time: 64.1 us -> 60.4 us (0.942)
  Pallas kernels: 62.6 us -> 58.9 us
    pallas_call x1, Pallas kernels: 58.9 us -> 55.2 us  [body(): pl.pallas_call(upper_kernel, name='upper', out_shape=(shape((2, 4, 4, 16,...]
where the time goes in v3:
time: 60.4 us; the launch traced here: 60.2 us
  Pallas kernels  58.9 us (98%)
  between operations  1.29 us (2%)
    pallas_call x1, Pallas kernels, body(): pl.pallas_call(upper_kernel, name='upper', out_shape=(shape((2, 4, 4, 16,...  55.2 us
    pallas_call x1, Pallas kernels, body(): pl.pallas_call(leaf_kernel, name='leaf_back', out_shape=(shape((1, LEAF_R...  3.74 us

profile of v3, /device:TPU:1, one launch (start us, length us, event | category | flops | bytes accessed | tf_op | source)
XLA Modules:
  0.0 60.2 jit_solution(12849561557282927923)
XLA Ops:
  1.3 55.2 %upper.1 = (bf16[2,4,4,16,1280]{4,3,2,1,0:T(8,128)(2,1)}, bf16[256,1024]{1,0:T(8,128)(2,1)}) custom-call(s32[1,256]{1,0:T(1,128)} %col_v.1, s32[1,256]{1,0:T(1,128)} %tgt_v.1, s32[1,1]{1,0:T(1,128)S(6)} %copy.18.cnt_s, f32[1,1024,256]{2,1,0:T(8,128)} %rhs_h.1, bf16[1,8,128,128]{3,2,1,0:T(8,128)(2,1)} %inv.1, bf16[1,256,128,128]{3,2,1,0:T(8,128)(2,1)} %tiles_h.1, ...), custom_call_target="tpu_custom_call" | custom-call | tf_op jit(solution)/shard_map/upper/pallas_call | solution.py:564
  56.5 3.7 %leaf_back.1 = (f32[1,1024,256]{2,1,0:T(8,128)}, f32[1,512,256]{2,1,0:T(8,128)}, f32[1024,256]{1,0:T(8,128)}, f32[1024,256]{1,0:T(8,128)}) custom-call(bf16[2,4,4,16,1280]{4,3,2,1,0:T(8,128)(2,1)} %get-tuple-element.6.ab, bf16[256,1024]{1,0:T(8,128)(2,1)} %get-tuple-element.7.back, bf16[1,8,128,128]{3,2,1,0:T(8,128)(2,1)} %inv.1), custom_call_target="tpu_custom_call" | custom-call | tf_op jit(solution)/shard_map/leaf_back/pallas_call | solution.py:615

commit v4 on v3

--- a/solution.py
+++ b/solution.py
@@ -137,15 +137,7 @@
     f_mp.wait()
     mpx[c] = mp8[...].astype(F32)
 
-    f_inv.wait()
-    f_rhs.wait()
-    for s in range(LEAF_SN):
-        rows = slice(s * BLOCK, (s + 1) * BLOCK)
-        solved = nn(inv[s], rhs[rows, :].astype(BF16)).astype(BF16)
-        xt[:, rows] = nt(unit, solved).astype(BF16)
-
     f_gp.wait()
-    f_plan.wait()
     pl.semaphore_wait(barrier, len(peers))
 
     class Ring:
@@ -188,21 +180,13 @@
                 out.append(share(self.block((self.me + 4 - d) % 4)))
             return out
 
-    gp_ay = Ring(
-        "y",
-        lambda i: gpf.at[z, i, gp_rows, 0:256],
-        lambda i: (gpf.at[z, i, gp_rows, 0:128], gpf.at[z, i, gp_rows, 128:256]),
-    )
+    gp_ay = Direct("y", lambda i: gpf.at[z, i, gp_rows, 0:256])
     gp_az = Ring(
         "z",
         lambda i: gpf.at[i, :, gp_rows, 0:256],
         lambda i: (gpf.at[i, :, gp_rows, 0:128], gpf.at[i, :, gp_rows, 128:256]),
     )
-    gp_bz = Ring(
-        "z",
-        lambda i: gpf.at[i, y, gp_rows, 256:512],
-        lambda i: (gpf.at[i, y, gp_rows, 256:384], gpf.at[i, y, gp_rows, 384:512]),
-    )
+    gp_bz = Direct("z", lambda i: gpf.at[i, y, gp_rows, 256:512])
     gp_by = Ring(
         "y",
         lambda i: gpf.at[:, i, gp_rows, 256:512],
@@ -220,6 +204,21 @@
     gp_ay.start()
     gp_bz.start()
 
+    f_inv.wait()
+    f_rhs.wait()
+    for s in range(LEAF_SN):
+        rows = slice(s * BLOCK, (s + 1) * BLOCK)
+        solved = nn(inv[s], rhs[rows, :].astype(BF16)).astype(BF16)
+        xt[:, rows] = nt(unit, solved).astype(BF16)
+
+    m_pair.wait_recv()
+    both = jnp.concatenate([mpx[0], mpx[1]], axis=0).astype(BF16)
+    mpt[0] = both[:, 0:512]
+    mpt[1] = both[:, 512:1024]
+    mpf[c, x, z, y] = mpt[c]
+    mp_z.start()
+
+    f_plan.wait()
     for copy in f_tiles:
         copy.wait()
     side = pl.ds(pl.multiple_of((y // 2) * 128, 128), 128)
@@ -242,23 +241,16 @@
 
     run[TILES] = jnp.zeros((BLOCK, BLOCK), BF16)
     total = lax.fori_loop(0, 16, add_tiles, jnp.zeros((BLOCK, BLOCK), F32))
-    m_pair.wait_recv()
-    both = jnp.concatenate([mpx[0], mpx[1]], axis=0).astype(BF16)
-    mpt[0] = both[:, 0:512]
-    mpt[1] = both[:, 512:1024]
-    mpf[c, x, z, y] = mpt[c]
-    mp_z.start()
-    total = lax.fori_loop(16, 32, add_tiles, total)
-    gp_ay.relay()
-    gp_bz.relay()
-    total = lax.fori_loop(32, 48, add_tiles, total)
-    mp_z.finish()
-    mp_y.start()
-    total = lax.fori_loop(48, 64, add_tiles, total)
     gp_ay.finish()
     gp_az.start()
     gp_bz.finish()
     gp_by.start()
+    s_gp = [share(ring.block(ring.me)) for ring in (gp_az, gp_by)]
+    total = lax.fori_loop(16, 32, add_tiles, total)
+    mp_z.finish()
+    mp_y.start()
+    total = lax.fori_loop(32, 48, add_tiles, total)
+    total = lax.fori_loop(48, 64, add_tiles, total)
 
     def dense(chunk):
         rows = []
@@ -359,27 +351,23 @@
     f_rt.wait()
     rt_t = columns(rt)
 
+    gp_az.relay()
+    gp_by.relay()
     for scatter in scatters:
         scatter.second()
-    gp_az.relay()
-    gp_by.relay()
-    s_gp = []
+    mp_x.relay()
     for ring in (gp_az, gp_by):
-        for d in (0, 3, 1):
+        for d in (3, 1):
             s_gp.append(share(ring.block((ring.me + d) % 4)))
-    mp_x.relay()
-    s_mp = [share(mp_x.block((x + d) % 4)) for d in (0, 3, 1)]
 
     gres[c] = (rg_t - scatters[0].finish()).astype(BF16)
     s_g = share(gres.at[c])
-    mid_half = scatters[1].finish()
-    top_half = scatters[2].finish()
+    for ring in (gp_az, gp_by):
+        ring.finish()
+        s_gp.append(share(ring.block((ring.me + 2) % 4)))
     f_ig.wait()
     s_g.wait_recv()
     group_solved = nt(jnp.concatenate([gres[0], gres[1]], axis=1), ig[...]).astype(BF16)
-    for ring in (gp_az, gp_by):
-        ring.finish()
-        s_gp.append(share(ring.block((ring.me + 2) % 4)))
     for copy in s_gp:
         copy.wait_recv()
 
@@ -398,14 +386,15 @@
             )
         return jnp.concatenate(halves, axis=1)
 
-    cross_m = cross(0, mid_half, c)
-    cross_t = cross(1, top_half, 2 + c)
+    cross_m = cross(0, scatters[1].finish(), c)
+    cross_t = cross(1, scatters[2].finish(), 2 + c)
+    s_mp = [share(mp_x.block((x + d) % 4)) for d in (0, 3, 1)]
+    mp_x.finish()
+    s_mp.append(share(mp_x.block((x + 2) % 4)))
     f_im.wait()
     for copy in cross_m:
         copy.wait_recv()
     mid_solved = nt((rm_t - total_of(0)).astype(BF16), im[...]).astype(BF16)
-    mp_x.finish()
-    s_mp.append(share(mp_x.block((x + 2) % 4)))
     for copy in s_mp:
         copy.wait_recv()
     below = nt(mid_solved[:, 0:512], mpf[0].reshape(1024, 512)) + nt(

time: 60.4 us -> 55.8 us (0.924)
  Pallas kernels: 58.9 us -> 54.3 us
    pallas_call x1, Pallas kernels: 55.2 us -> 50.6 us  [body(): pl.pallas_call(upper_kernel, name='upper', out_shape=(shape((2, 4, 4, 16,...]
where the time goes in v4:
time: 55.8 us; the launch traced here: 55.6 us
  Pallas kernels  54.3 us (97%)
  between operations  1.29 us (2%)
    pallas_call x1, Pallas kernels, body(): pl.pallas_call(upper_kernel, name='upper', out_shape=(shape((2, 4, 4, 16,...  50.6 us
    pallas_call x1, Pallas kernels, body(): pl.pallas_call(leaf_kernel, name='leaf_back', out_shape=(shape((1, LEAF_R...  3.74 us

profile of v4, /device:TPU:1, one launch (start us, length us, event | category | flops | bytes accessed | tf_op | source)
XLA Modules:
  0.0 55.6 jit_solution(6119283506870952996)
XLA Ops:
  1.3 50.6 %upper.1 = (bf16[2,4,4,16,1280]{4,3,2,1,0:T(8,128)(2,1)}, bf16[256,1024]{1,0:T(8,128)(2,1)}) custom-call(s32[1,256]{1,0:T(1,128)} %col_v.1, s32[1,256]{1,0:T(1,128)} %tgt_v.1, s32[1,1]{1,0:T(1,128)S(6)} %copy.18.cnt_s, f32[1,1024,256]{2,1,0:T(8,128)} %rhs_h.1, bf16[1,8,128,128]{3,2,1,0:T(8,128)(2,1)} %inv.1, bf16[1,256,128,128]{3,2,1,0:T(8,128)(2,1)} %tiles_h.1, ...), custom_call_target="tpu_custom_call" | custom-call | tf_op jit(solution)/shard_map/upper/pallas_call | solution.py:553
  51.9 3.7 %leaf_back.1 = (f32[1,1024,256]{2,1,0:T(8,128)}, f32[1,512,256]{2,1,0:T(8,128)}, f32[1024,256]{1,0:T(8,128)}, f32[1024,256]{1,0:T(8,128)}) custom-call(bf16[2,4,4,16,1280]{4,3,2,1,0:T(8,128)(2,1)} %get-tuple-element.6.ab, bf16[256,1024]{1,0:T(8,128)(2,1)} %get-tuple-element.7.back, bf16[1,8,128,128]{3,2,1,0:T(8,128)(2,1)} %inv.1), custom_call_target="tpu_custom_call" | custom-call | tf_op jit(solution)/shard_map/leaf_back/pallas_call | solution.py:604

commit v5 on v4

--- a/solution.py
+++ b/solution.py
@@ -16,7 +16,6 @@
 BF16 = jnp.bfloat16
 ANY = pl.BlockSpec(memory_space=pl.ANY)
 VMEM_IN = pl.BlockSpec(memory_space=pltpu.VMEM)
-SMEM_IN = pl.BlockSpec(memory_space=pltpu.SMEM)
 VMEM_LIMIT = 60 * 1024 * 1024
 
 GROUP_SEG = (0, 256)
@@ -46,9 +45,9 @@
 
 
 def upper_kernel(
-    col_v, tgt_v, cnt_s, rhs_h, inv_h, tiles_h, rg_h, rm_h, rt_h, ig_h, im_h, it_h, gp_h, mp_h,
+    col_h, tgt_h, cnt_h, rhs_h, inv_h, tiles_h, rg_h, rm_h, rt_h, ig_h, im_h, it_h, gp_h, mp_h,
     ab_h, back_h,
-    rhs, inv, tiles, run, plan_v, plan_s, xt, rg, rm, rt, ig, im, it, mp8, mpx, mpt, gpf, mpf,
+    col_v, tgt_v, cnt_v, rhs, inv, tiles, run, plan_v, plan_s, xt, rg, rm, rt, ig, im, it, mp8, mpx, mpt, gpf, mpf,
     ps, prx, s_, ya, zb, ta, tb, za, yb,
     gres, xr, stage_t, stage_g, ab, back,
     lsem, ssem, rsem,
@@ -103,11 +102,14 @@
     gp_rows = pl.ds(pl.multiple_of(c * 64, 64), 64)
     f_gp = fetch(gp_h.at[0], gpf.at[z, y, gp_rows, :])
     f_mp = fetch(mp_h, mp8)
+    f_slots = [fetch(col_h, col_v), fetch(tgt_h, tgt_v), fetch(cnt_h, cnt_v)]
     f_inv = fetch(inv_h.at[0], inv)
     f_rhs = fetch(rhs_h.at[0], rhs)
     f_tiles = [fetch(tiles_h.at[0, pl.ds(i * 64, 64)], tiles.at[pl.ds(i * 64, 64)]) for i in range(4)]
 
-    count = cnt_s[0, 0]
+    for copy in f_slots:
+        copy.wait()
+    count = cnt_v[...]
     unit = eye(RHS)
     lane = lax.broadcasted_iota(jnp.int32, (1, TILES), 1)
     key = jnp.where(lane < count, place_of(tgt_v[...]) * LEAF_SN + col_v[...], 255).astype(F32)
@@ -231,7 +233,7 @@
 
     def add_tile(p, total):
         total = total * plan_s[1, p].astype(F32) + tiles[plan_s[0, p]].astype(F32)
-        run[p] = total.astype(BF16)
+        run[p] = total
         return total
 
     def add_tiles(i, total):
@@ -239,7 +241,7 @@
             total = add_tile(i * 4 + q, total)
         return total
 
-    run[TILES] = jnp.zeros((BLOCK, BLOCK), BF16)
+    run[TILES] = jnp.zeros((BLOCK, BLOCK), F32)
     total = lax.fori_loop(0, 16, add_tiles, jnp.zeros((BLOCK, BLOCK), F32))
     gp_ay.finish()
     gp_az.start()
@@ -256,7 +258,7 @@
         rows = []
         for r in range(2):
             spots = [plan_s[2, (chunk * 2 + r) * LEAF_SN + s] for s in range(LEAF_SN)]
-            rows.append(jnp.concatenate([run[spot] for spot in spots], axis=1))
+            rows.append(jnp.concatenate([run[spot].astype(BF16) for spot in spots], axis=1))
         return jnp.concatenate(rows, axis=0)
 
     class Scatter:
@@ -360,6 +362,7 @@
         for d in (3, 1):
             s_gp.append(share(ring.block((ring.me + d) % 4)))
 
+    early = len(sent)
     gres[c] = (rg_t - scatters[0].finish()).astype(BF16)
     s_g = share(gres.at[c])
     for ring in (gp_az, gp_by):
@@ -392,6 +395,8 @@
     mp_x.finish()
     s_mp.append(share(mp_x.block((x + 2) % 4)))
     f_im.wait()
+    for copy in sent[:early]:
+        copy.wait_send()
     for copy in cross_m:
         copy.wait_recv()
     mid_solved = nt((rm_t - total_of(0)).astype(BF16), im[...]).astype(BF16)
@@ -504,10 +509,10 @@
     rest = settle(1)
     back[...] = rest.astype(BF16)
     out.append(fetch(back, back_h))
+    for copy in sent[early:]:
+        copy.wait_send()
     for copy in out:
         copy.wait()
-    for copy in sent:
-        copy.wait_send()
 
 
 def leaf_kernel(ab, back, inv, leaf_h, group_h, mid_h, top_h, leaf_v, group_v, mid_v, top_v, osem):
@@ -554,13 +559,16 @@
         upper_kernel,
         name="upper",
         out_shape=(shape((2, 4, 4, 16, HALF), BF16), shape((RHS, LEAF_ROWS), BF16)),
-        in_specs=[VMEM_IN, VMEM_IN, SMEM_IN] + [ANY] * 11,
+        in_specs=[ANY] * 14,
         out_specs=(ANY, ANY),
         scratch_shapes=[
+            vm((1, TILES), jnp.int32),
+            vm((1, TILES), jnp.int32),
+            vm((1, 1), jnp.int32),
             vm((LEAF_ROWS, RHS), F32),
             vm((LEAF_SN, BLOCK, BLOCK), BF16),
             vm((TILES, BLOCK, BLOCK), BF16),
-            vm((TILES + 1, BLOCK, BLOCK), BF16),
+            vm((TILES + 1, BLOCK, BLOCK), F32),
             vm((8, TILES), jnp.int32),
             pltpu.SMEM((8, TILES), jnp.int32),
             vm((RHS, LEAF_ROWS), BF16),
@@ -590,7 +598,7 @@
             vm((2, 16, 256), BF16),
             vm((2, 4, 4, 16, HALF), BF16),
             vm((RHS, LEAF_ROWS), BF16),
-            pltpu.SemaphoreType.DMA((24,)),
+            pltpu.SemaphoreType.DMA((28,)),
             pltpu.SemaphoreType.DMA((180,)),
             pltpu.SemaphoreType.DMA((180,)),
         ],

time: 55.8 us -> 55 us (0.986)
  Pallas kernels: 54.3 us -> 53.6 us
    pallas_call x1, Pallas kernels: 50.6 us -> 49.9 us  [body(): pl.pallas_call(upper_kernel, name='upper', out_shape=(shape((2, 4, 4, 16,...]
where the time goes in v5:
time: 55 us; the launch traced here: 54.9 us
  Pallas kernels  53.6 us (97%)
  between operations  1.29 us (2%)
    pallas_call x1, Pallas kernels, body(): pl.pallas_call(upper_kernel, name='upper', out_shape=(shape((2, 4, 4, 16,...  49.9 us
    pallas_call x1, Pallas kernels, body(): pl.pallas_call(leaf_kernel, name='leaf_back', out_shape=(shape((1, LEAF_R...  3.74 us

profile of v5, /device:TPU:1, one launch (start us, length us, event | category | flops | bytes accessed | tf_op | source)
XLA Modules:
  0.0 54.9 jit_solution(13992424334639254219)
XLA Ops:
  1.3 49.9 %upper.1 = (bf16[2,4,4,16,1280]{4,3,2,1,0:T(8,128)(2,1)}, bf16[256,1024]{1,0:T(8,128)(2,1)}) custom-call(s32[1,256]{1,0:T(1,128)} %col_h.1, s32[1,256]{1,0:T(1,128)} %tgt_h.1, s32[1,1]{1,0:T(1,128)S(6)} %copy.18.cnt_h, f32[1,1024,256]{2,1,0:T(8,128)} %rhs_h.1, bf16[1,8,128,128]{3,2,1,0:T(8,128)(2,1)} %inv.1, bf16[1,256,128,128]{3,2,1,0:T(8,128)(2,1)} %tiles_h.1, ...), custom_call_target="tpu_custom_call" | custom-call | tf_op jit(solution)/shard_map/upper/pallas_call | solution.py:558
  51.1 3.7 %leaf_back.1 = (f32[1,1024,256]{2,1,0:T(8,128)}, f32[1,512,256]{2,1,0:T(8,128)}, f32[1024,256]{1,0:T(8,128)}, f32[1024,256]{1,0:T(8,128)}) custom-call(bf16[2,4,4,16,1280]{4,3,2,1,0:T(8,128)(2,1)} %get-tuple-element.6.ab, bf16[256,1024]{1,0:T(8,128)(2,1)} %get-tuple-element.7.back, bf16[1,8,128,128]{3,2,1,0:T(8,128)(2,1)} %inv.1), custom_call_target="tpu_custom_call" | custom-call | tf_op jit(solution)/shard_map/leaf_back/pallas_call | solution.py:612

commit v6 on v5

--- a/solution.py
+++ b/solution.py
@@ -237,22 +237,22 @@
         return total
 
     def add_tiles(i, total):
-        for q in range(4):
-            total = add_tile(i * 4 + q, total)
+        for q in range(8):
+            total = add_tile(i * 8 + q, total)
         return total
 
     run[TILES] = jnp.zeros((BLOCK, BLOCK), F32)
-    total = lax.fori_loop(0, 16, add_tiles, jnp.zeros((BLOCK, BLOCK), F32))
+    total = lax.fori_loop(0, 8, add_tiles, jnp.zeros((BLOCK, BLOCK), F32))
     gp_ay.finish()
     gp_az.start()
     gp_bz.finish()
     gp_by.start()
     s_gp = [share(ring.block(ring.me)) for ring in (gp_az, gp_by)]
-    total = lax.fori_loop(16, 32, add_tiles, total)
+    total = lax.fori_loop(8, 16, add_tiles, total)
     mp_z.finish()
     mp_y.start()
-    total = lax.fori_loop(32, 48, add_tiles, total)
-    total = lax.fori_loop(48, 64, add_tiles, total)
+    total = lax.fori_loop(16, 24, add_tiles, total)
+    total = lax.fori_loop(24, 32, add_tiles, total)
 
     def dense(chunk):
         rows = []

time: 55 us -> 55.2 us (level)
  no operation moved by 1% of the time
where the time goes in v6:
time: 55.2 us; the launch traced here: 55.1 us
  Pallas kernels  53.8 us (97%)
  between operations  1.29 us (2%)
    pallas_call x1, Pallas kernels, body(): pl.pallas_call(upper_kernel, name='upper', out_shape=(shape((2, 4, 4, 16,...  50 us
    pallas_call x1, Pallas kernels, body(): pl.pallas_call(leaf_kernel, name='leaf_back', out_shape=(shape((1, LEAF_R...  3.74 us

profile of v6, /device:TPU:1, one launch (start us, length us, event | category | flops | bytes accessed | tf_op | source)
XLA Modules:
  0.0 55.1 jit_solution(3766066298057791329)
XLA Ops:
  1.3 50.0 %upper.1 = (bf16[2,4,4,16,1280]{4,3,2,1,0:T(8,128)(2,1)}, bf16[256,1024]{1,0:T(8,128)(2,1)}) custom-call(s32[1,256]{1,0:T(1,128)} %col_h.1, s32[1,256]{1,0:T(1,128)} %tgt_h.1, s32[1,1]{1,0:T(1,128)S(6)} %copy.18.cnt_h, f32[1,1024,256]{2,1,0:T(8,128)} %rhs_h.1, bf16[1,8,128,128]{3,2,1,0:T(8,128)(2,1)} %inv.1, bf16[1,256,128,128]{3,2,1,0:T(8,128)(2,1)} %tiles_h.1, ...), custom_call_target="tpu_custom_call" | custom-call | tf_op jit(solution)/shard_map/upper/pallas_call | solution.py:558
  51.3 3.7 %leaf_back.1 = (f32[1,1024,256]{2,1,0:T(8,128)}, f32[1,512,256]{2,1,0:T(8,128)}, f32[1024,256]{1,0:T(8,128)}, f32[1024,256]{1,0:T(8,128)}) custom-call(bf16[2,4,4,16,1280]{4,3,2,1,0:T(8,128)(2,1)} %get-tuple-element.6.ab, bf16[256,1024]{1,0:T(8,128)(2,1)} %get-tuple-element.7.back, bf16[1,8,128,128]{3,2,1,0:T(8,128)(2,1)} %inv.1), custom_call_target="tpu_custom_call" | custom-call | tf_op jit(solution)/shard_map/leaf_back/pallas_call | solution.py:612
